TPU v7x, 128 devices: a whole 4x4x4 slice. The times are simulated.
128 devices in a mesh: frame: 4 (over x), pix: 32 (over y, z, core).
Axes of the slice: x: 4, y: 4, z: 4, core: 2. Of those that a mesh axis runs over, the one named last changes fastest.
Arguments:
- frames: bfloat16 [128, 4, 512, 512], P('frame', None, 'pix'), may hold values from -26 to 26
- prev_fg: bfloat16 [128, 4, 512, 512], P('frame', None, 'pix'), may hold values from -3 to 3
- depth_valid: int32 [128, 512, 512], P('frame', 'pix'), may hold values 0 or 1
- sketch: float32 [128, 64], replicated, may hold values from -0.5 to 0.5
- tv_weight: float32 [4], replicated, may hold values from 0.1 to 1
Outputs:
- background: bfloat16 [128, 4, 512, 512], P('frame', None, 'pix')
- foreground: bfloat16 [128, 4, 512, 512], P('frame', None, 'pix')
All inputs are finite; a program needn't handle non-finite values. No bound on the sum of `depth_valid` on one device may be relied on, other than what follows from the above.
Results may differ from a plain program's by a relative error of at most 0.012.
The roundings to bfloat16 on the way count: a program that leaves them out, or rounds other values in their place, can miss the bound.
Values may be sent and summed in bfloat16 or wider, within the bound.
A program may use at most 64 MiB of HBM per device.

v0:
```python
import jax
import jax.numpy as jnp
from jax import lax
from jax.sharding import PartitionSpec as P

POWER = 3
NSWEEP = 5


STEP_SIZE = 0.125


def shortened(shard):

    def short(part):
        return part.astype(jnp.bfloat16) if part.dtype == jnp.float32 else part

    return jax.tree.map(short, shard)


def from_behind(value, axis, steps):
    count = lax.axis_size(axis)
    leading, last = (max(0, -steps), min(count, count - steps))
    return lax.ppermute(value, axis, [(source, source + steps) for source in range(leading, last)])


def exact_dot(left, right):
    return jnp.dot(left, right, precision=lax.Precision.HIGHEST)


def mixing_matrix(gram, sketch):
    basis = sketch
    for turn in range(POWER):
        image = exact_dot(gram, basis)
        factor = jnp.linalg.cholesky(exact_dot(basis.T, image))
        basis = lax.linalg.triangular_solve(
            factor, image, left_side=False, lower=True, transpose_a=True
        )
    image = exact_dot(gram, basis)
    factor = jnp.linalg.cholesky(exact_dot(basis.T, image))
    middle = lax.linalg.triangular_solve(
        factor, exact_dot(basis.T, gram), left_side=True, lower=True
    )
    coeffs = lax.linalg.triangular_solve(
        factor, middle, left_side=True, lower=True, transpose_a=True
    )
    return exact_dot(basis, coeffs)


def pair_rows(left, right):
    return lax.dot_general(
        left, right, (((1,), (1,)), ((), ())), preferred_element_type=jnp.float32
    )


def over_frames(weights, pixels):
    return lax.dot_general(
        weights, pixels, (((0,), (0,)), ((), ())), preferred_element_type=jnp.float32
    )


def dual_update(first, second, down, across, step):
    size = jnp.sqrt(down * down + across * across)
    scale = 1.0 + step * size
    return ((first - step * down) / scale, (second - step * across) / scale)


def col_prev(field):
    return jnp.pad(field[:, :, :, :-1], ((0, 0), (0, 0), (0, 0), (1, 0)))


def col_grad(smooth, last_col):
    next_cols = jnp.pad(smooth[:, :, :, 1:], ((0, 0), (0, 0), (0, 0), (0, 1)))
    return jnp.where(last_col, 0.0, next_cols - smooth)


def local(frames, prev_fg, depth_valid, sketch, tv_weight):
    count, chans, rows, cols = frames.shape
    height = rows * lax.axis_size("pix")
    nval = chans * height * cols
    start_frame = lax.axis_index("frame") * count
    chan_ids = lax.broadcasted_iota(jnp.int32, (1, chans, 1, 1), 1)
    depth_ok = depth_valid[:, None, :, :].astype(jnp.float32)
    valid = jnp.where(chan_ids == chans - 1, depth_ok, jnp.float32(1.0))
    resid = ((frames.astype(jnp.float32) - prev_fg.astype(jnp.float32)) * valid).astype(
        jnp.bfloat16
    )
    flat = resid.reshape(count, chans * rows * cols)
    everyone = lax.all_gather(flat, "frame", axis=0, tiled=True)
    block = pair_rows(everyone, flat)
    summed = lax.psum(block, "pix")
    gram = lax.all_gather(summed, "frame", axis=1, tiled=True)
    gram = gram / nval
    mixing = mixing_matrix(gram, sketch)
    mine = lax.dynamic_slice_in_dim(mixing, start_frame, count, 1).astype(jnp.bfloat16)
    back = over_frames(mine, everyone)
    background = back.reshape(count, chans, rows, cols).astype(jnp.bfloat16)
    rounded = lax.optimization_barrier(background).astype(jnp.float32)
    source = (frames.astype(jnp.float32) - rounded) * valid
    lam = tv_weight.reshape(1, chans, 1, 1)
    step = STEP_SIZE / lam
    last_col = lax.broadcasted_iota(jnp.int32, (1, 1, 1, cols), 3) == cols - 1
    row_ids = lax.axis_index("pix") * rows + lax.broadcasted_iota(jnp.int32, (1, 1, rows, 1), 2)
    last_row = row_ids == height - 1

    def divergence(first, second):
        above = from_behind(shortened(first[:, :, -1:, :]), "pix", 1)
        prev_rows = jnp.concatenate([above, first[:, :, :-1, :]], axis=2)
        return first - prev_rows + (second - col_prev(second))

    first = jnp.zeros_like(source)
    second = jnp.zeros_like(source)
    for sweep in range(NSWEEP):
        smooth = source - lam * divergence(first, second)
        below = from_behind(shortened(smooth[:, :, :1, :]), "pix", -1)
        next_rows = jnp.concatenate([smooth[:, :, 1:, :], below], axis=2)
        down = jnp.where(last_row, 0.0, next_rows - smooth)
        across = col_grad(smooth, last_col)
        first, second = dual_update(first, second, down, across, step)
    smooth = source - lam * divergence(first, second)
    return (background, smooth.astype(jnp.bfloat16))


def solution(mesh):
    placed = (
        P("frame", None, "pix", None),
        P("frame", None, "pix", None),
        P("frame", "pix", None),
        P(),
        P(),
    )
    return jax.shard_map(
        local,
        mesh=mesh,
        in_specs=placed,
        out_specs=(P("frame", None, "pix", None), P("frame", None, "pix", None)),
        check_vma=False,
    )
```

profile of v0, /device:TPU:8, one launch (start us, length us, event | category | flops | bytes accessed | tf_op | source)
XLA Modules:
  0.0 442.0 jit_solution(11430136703876754686)
XLA Ops:
  9.7 3.6 fusion
  17.5 82.8 %all-gather.2.cloned.1.call-done = bf16[128,32768]{1,0:T(8,128)(2,1)} async-done(((bf16[32,32768]{1,0:T(8,128)(2,1)}), bf16[128,32768]{1,0:T(8,128)(2,1)}) %all-gather.2.cloned.1.call-update) | async-done | bytes 8388624 | tf_op jit(solution)/shard_map/all_gather | solution.py:89
  100.3 6.9 %fusion.61 = f32[128,32]{0,1:T(8,128)S(1)} fusion(bf16[128,32768]{1,0:T(8,128)(2,1)} %all-gather.2.cloned.1.call-done, bf16[32,32768]{1,0:T(8,128)(2,1)} %bitcast.91), kind=kOutput, calls=%fused_computation.132 | convolution fusion | flops 268435456 | bytes 10502144 | tf_op jit(solution)/shard_map/dot_general | solution.py:51
  107.2 110.5 %psum.7 = f32[128,32]{0,1:T(8,128)S(1)} all-reduce(f32[128,32]{0,1:T(8,128)S(1)} %fusion.61), channel_id=1, replica_groups=mesh['frame'=4,'pix'=32] {'pix'}, use_global_device_ids=true, to_apply=%region_0.1 | all-reduce | flops 4096 | bytes 32768 | tf_op jit(solution)/shard_map/psum | solution.py:91
  217.7 12.0 %all_gather.7 = f32[128,128]{0,1:T(8,128)S(1)} all-gather(f32[128,32]{0,1:T(8,128)S(1)} %psum.7), channel_id=1, replica_groups=mesh['frame'=4,'pix'=32] {'frame'}, dimensions={1}, use_global_device_ids=true | all-gather | bytes 81920 | tf_op jit(solution)/shard_map/all_gather | solution.py:92
  230.2 5.8 %cholesky.74 = f32[64,64]{1,0:T(8,128)S(1)} custom-call(f32[64,64]{1,0:T(8,128)S(1)} %add_multiply_fusion), custom_call_target="Cholesky" | custom-call | tf_op jit(solution)/shard_map/jit(cholesky)/cholesky | solution.py:35
  237.4 4.9 %custom-call.13 = f32[1,64,64]{1,2,0:T(8,128)S(1)} custom-call(f32[1,64,64]{2,1,0:T(8,128)S(1)} %fusion.32), custom_call_target="InvertDiagBlocksLowerTriangular" | custom-call | tf_op jit(solution)/shard_map/triangular_solve/custom-call.0 | solution.py:36
  243.0 5.8 %cholesky.85 = f32[64,64]{1,0:T(8,128)S(1)} custom-call(f32[64,64]{1,0:T(8,128)S(1)} %fusion.44), custom_call_target="Cholesky" | custom-call | tf_op jit(solution)/shard_map/jit(cholesky)/cholesky | solution.py:35
  250.2 4.9 %custom-call.14 = f32[1,64,64]{1,2,0:T(8,128)S(1)} custom-call(f32[1,64,64]{2,1,0:T(8,128)S(1)} %fusion.33), custom_call_target="InvertDiagBlocksLowerTriangular" | custom-call | tf_op jit(solution)/shard_map/triangular_solve/custom-call.0 | solution.py:36
  255.8 5.8 %cholesky.96 = f32[64,64]{1,0:T(8,128)S(1)} custom-call(f32[64,64]{1,0:T(8,128)S(1)} %fusion.42), custom_call_target="Cholesky" | custom-call | tf_op jit(solution)/shard_map/jit(cholesky)/cholesky | solution.py:35
  263.0 4.9 %custom-call.15 = f32[1,64,64]{1,2,0:T(8,128)S(1)} custom-call(f32[1,64,64]{2,1,0:T(8,128)S(1)} %fusion.34), custom_call_target="InvertDiagBlocksLowerTriangular" | custom-call | tf_op jit(solution)/shard_map/triangular_solve/custom-call.0 | solution.py:36
  268.9 5.8 %cholesky.107 = f32[64,64]{1,0:T(8,128)S(1)} custom-call(f32[64,64]{1,0:T(8,128)S(1)} %fusion.40), custom_call_target="Cholesky" | custom-call | tf_op jit(solution)/shard_map/jit(cholesky)/cholesky | solution.py:40
  276.1 4.9 %custom-call.10 = f32[1,64,64]{1,2,0:T(8,128)S(1)} custom-call(f32[1,64,64]{2,1,0:T(8,128)S(1)} %fusion.35), custom_call_target="InvertDiagBlocksLowerTriangular" | custom-call | tf_op jit(solution)/shard_map/triangular_solve | solution.py:44
  281.7 4.6 %convolution_convert_fusion = bf16[32,32768]{1,0:T(8,128)(2,1)S(1)} fusion(bf16[128,32768]{1,0:T(8,128)(2,1)} %all-gather.2.cloned.1.call-done, bf16[128,128]{0,1:T(8,128)(2,1)S(1)} %fusion.66, s32[]{:T(128)S(6)} %select_n.43), kind=kOutput, calls=%fused_computation | convolution fusion | flops 269484032 | bytes 10493956 | tf_op jit(solution)/shard_map/dot_general | solution.py:57
  287.1 3.5 multiply_subtract_fusion
  298.7 3.6 subtract_divide_fusion.8
  305.6 7.1 %collective-permute-done.2 = bf16[32,4,1,512]{3,0,2,1:T(8,128)(2,1)S(1)} collective-permute-done((bf16[32,4,1,512]{3,0,2,1:T(8,128)(2,1)S(1)}, bf16[32,4,1,512]{3,0,2,1:T(8,128)(2,1)S(1)}, u32[]{:S(2)}, u32[]{:S(2)}) %collective-permute-start.2) | collective-permute-done | bytes 131104 | tf_op jit(solution)/shard_map/ppermute | solution.py:24
  312.8 5.2 %fusion.4 = f32[32,4,16,512]{3,0,2,1:T(8,128)S(1)} fusion(f32[32,4,16,512]{3,0,2,1:T(8,128)S(1)} %get-tuple-element.17, f32[32,4,15,512]{3,0,2,1:T(8,128)S(1)} %slice.153, f32[32,4,1,512]{3,0,2,1:T(8,128)S(1)} %convert_element_type.96, f32[32,4,16,512]{3,0,2,1:T(8,128)S(1)} %get-tuple-element.16, f32[32,4,16,511]{3,0,2,1:T(8,128)S(1)} %bitcast.88, ...), kind=kLoop, calls=%fused_computation.11 | loop fusion | flops 11534336 | bytes 26206228 | tf_op jit(solution)/shard_map/sub | solution.py:114
  322.5 3.1 slice.157
  325.7 5.9 %subtract_divide_fusion.6 = (f32[32,4,16,512]{3,0,2,1:T(8,128)S(1)}, f32[32,4,16,512]{3,0,2,1:T(8,128)S(1)}) fusion(f32[32,4,16,512]{3,0,2,1:T(8,128)S(1)} %get-tuple-element.16, f32[4]{0:T(128)S(1)} %broadcast_divide_fusion, f32[32,4,16,512]{3,0,2,1:T(8,128)S(1)} %fusion.4, f32[32,4,16,511]{3,0,2,1:T(8,128)} %slice.157, ...), kind=kLoop, calls=%fused_computation.49 | loop fusion | flops 16777216 | bytes 29352480 | tf_op jit(solution)/shard_map/div | solution.py:65
  335.1 6.7 %collective-permute-done.4 = bf16[32,4,1,512]{3,0,2,1:T(8,128)(2,1)S(1)} collective-permute-done((bf16[32,4,1,512]{3,0,2,1:T(8,128)(2,1)S(1)}, bf16[32,4,1,512]{3,0,2,1:T(8,128)(2,1)S(1)}, u32[]{:S(2)}, u32[]{:S(2)}) %collective-permute-start.4) | collective-permute-done | bytes 131104 | tf_op jit(solution)/shard_map/ppermute | solution.py:24
  341.8 5.2 %fusion.8 = f32[32,4,16,512]{3,0,2,1:T(8,128)S(1)} fusion(f32[32,4,16,512]{3,0,2,1:T(8,128)S(1)} %get-tuple-element.15, f32[32,4,15,512]{3,0,2,1:T(8,128)S(1)} %slice.159, f32[32,4,1,512]{3,0,2,1:T(8,128)S(1)} %convert_element_type.98, f32[32,4,16,512]{3,0,2,1:T(8,128)S(1)} %get-tuple-element.14, f32[32,4,16,511]{3,0,2,1:T(8,128)S(1)} %bitcast.86, ...), kind=kLoop, calls=%fused_computation.17 | loop fusion | flops 11534336 | bytes 26206228 | tf_op jit(solution)/shard_map/sub | solution.py:114
  351.6 3.1 slice.163
  354.7 5.9 %subtract_divide_fusion.4 = (f32[32,4,16,512]{3,0,2,1:T(8,128)S(1)}, f32[32,4,16,512]{3,0,2,1:T(8,128)S(1)}) fusion(f32[32,4,16,512]{3,0,2,1:T(8,128)S(1)} %get-tuple-element.14, f32[4]{0:T(128)S(1)} %broadcast_divide_fusion, f32[32,4,16,512]{3,0,2,1:T(8,128)S(1)} %fusion.8, f32[32,4,16,511]{3,0,2,1:T(8,128)} %slice.163, ...), kind=kLoop, calls=%fused_computation.45 | loop fusion | flops 16777216 | bytes 29352480 | tf_op jit(solution)/shard_map/div | solution.py:65
  363.8 7.1 %collective-permute-done.6 = bf16[32,4,1,512]{3,0,2,1:T(8,128)(2,1)S(1)} collective-permute-done((bf16[32,4,1,512]{3,0,2,1:T(8,128)(2,1)S(1)}, bf16[32,4,1,512]{3,0,2,1:T(8,128)(2,1)S(1)}, u32[]{:S(2)}, u32[]{:S(2)}) %collective-permute-start.6) | collective-permute-done | bytes 131104 | tf_op jit(solution)/shard_map/ppermute | solution.py:24
  370.9 5.2 %fusion.12 = f32[32,4,16,512]{3,0,2,1:T(8,128)S(1)} fusion(f32[32,4,16,512]{3,0,2,1:T(8,128)S(1)} %get-tuple-element.13, f32[32,4,15,512]{3,0,2,1:T(8,128)S(1)} %slice.165, f32[32,4,1,512]{3,0,2,1:T(8,128)S(1)} %convert_element_type.100, f32[32,4,16,512]{3,0,2,1:T(8,128)S(1)} %get-tuple-element.12, f32[32,4,16,511]{3,0,2,1:T(8,128)S(1)} %bitcast.87, ...), kind=kLoop, calls=%fused_computation.23 | loop fusion | flops 11534336 | bytes 26206228 | tf_op jit(solution)/shard_map/sub | solution.py:114
  383.9 5.9 %subtract_divide_fusion.2 = (f32[32,4,16,512]{3,0,2,1:T(8,128)S(1)}, f32[32,4,16,512]{3,0,2,1:T(8,128)S(1)}) fusion(f32[32,4,16,512]{3,0,2,1:T(8,128)S(1)} %get-tuple-element.12, f32[4]{0:T(128)S(1)} %broadcast_divide_fusion, f32[32,4,16,512]{3,0,2,1:T(8,128)S(1)} %fusion.12, f32[32,4,16,511]{3,0,2,1:T(8,128)} %slice.169, ...), kind=kLoop, calls=%fused_computation.41 | loop fusion | flops 16777216 | bytes 29352480 | tf_op jit(solution)/shard_map/div | solution.py:65
  393.0 7.1 %collective-permute-done.8 = bf16[32,4,1,512]{3,0,2,1:T(8,128)(2,1)S(1)} collective-permute-done((bf16[32,4,1,512]{3,0,2,1:T(8,128)(2,1)S(1)}, bf16[32,4,1,512]{3,0,2,1:T(8,128)(2,1)S(1)}, u32[]{:S(2)}, u32[]{:S(2)}) %collective-permute-start.8) | collective-permute-done | bytes 131104 | tf_op jit(solution)/shard_map/ppermute | solution.py:24
  400.1 5.2 %fusion.16 = f32[32,4,16,512]{3,0,2,1:T(8,128)S(1)} fusion(f32[32,4,16,512]{3,0,2,1:T(8,128)S(1)} %get-tuple-element.11, f32[32,4,15,512]{3,0,2,1:T(8,128)S(1)} %slice.171, f32[32,4,1,512]{3,0,2,1:T(8,128)S(1)} %convert_element_type.102, f32[32,4,16,512]{3,0,2,1:T(8,128)S(1)} %get-tuple-element.10, f32[32,4,16,511]{3,0,2,1:T(8,128)S(1)} %bitcast.85, ...), kind=kLoop, calls=%fused_computation.29 | loop fusion | flops 11534336 | bytes 26206228 | tf_op jit(solution)/shard_map/sub | solution.py:114
  413.0 5.9 %subtract_divide_fusion = (f32[32,4,16,512]{3,0,2,1:T(8,128)S(1)}, f32[32,4,16,512]{3,0,2,1:T(8,128)S(1)}) fusion(f32[32,4,16,512]{3,0,2,1:T(8,128)S(1)} %get-tuple-element.10, f32[4]{0:T(128)S(1)} %broadcast_divide_fusion, f32[32,4,16,512]{3,0,2,1:T(8,128)S(1)} %fusion.16, f32[32,4,16,511]{3,0,2,1:T(8,128)} %slice.175, ...), kind=kLoop, calls=%fused_computation.37 | loop fusion | flops 16777216 | bytes 29352480 | tf_op jit(solution)/shard_map/div | solution.py:65
  422.3 5.0 %collective-permute-done.10 = bf16[32,4,1,512]{3,0,2,1:T(8,128)(2,1)S(1)} collective-permute-done((bf16[32,4,1,512]{3,0,2,1:T(8,128)(2,1)S(1)}, bf16[32,4,1,512]{3,0,2,1:T(8,128)(2,1)S(1)}, u32[]{:S(2)}, u32[]{:S(2)}) %collective-permute-start.10) | collective-permute-done | bytes 131104 | tf_op jit(solution)/shard_map/ppermute | solution.py:24
  427.3 5.1 %fusion.21 = bf16[32,4,16,512]{3,0,2,1:T(8,128)(2,1)S(1)} fusion(f32[32,4,16,512]{3,0,2,1:T(8,128)S(1)} %get-tuple-element.9, f32[32,4,15,512]{3,0,2,1:T(8,128)S(1)} %slice.177, f32[32,4,1,512]{3,0,2,1:T(8,128)S(1)} %convert_element_type.104, f32[32,4,16,512]{3,0,2,1:T(8,128)S(1)} %get-tuple-element.8, f32[32,4,16,511]{3,0,2,1:T(8,128)S(1)} %bitcast.89, ...), kind=kLoop, calls=%fused_computation.36 | loop fusion | flops 12582912 | bytes 24109076 | tf_op jit(solution)/shard_map/convert_element_type | solution.py:121
  (118 shorter events, 68.0 us)
Async XLA Ops:
  7.2 222.6 %copy-start = (f32[128,64]{0,1:T(8,128)S(1)}, f32[128,64]{0,1:T(8,128)}, u32[]{:S(2)}) copy-start(f32[128,64]{0,1:T(8,128)} %param.11) | copy-start | bytes 98308
  7.2 2.2 copy-start.2
  7.2 93.1 %all-gather.2.cloned.1.call-start = ((), (), s32[]{:S(2)}) async-start(), calls=%async_computation | async-start | bytes 10485760 | tf_op jit(solution)/shard_map/all_gather | solution.py:89
  7.2 2.5 copy-start.7
  13.3 4.2 copy-start.8
  15.5 271.5 %collective-permute-start = (bf16[32,4,1,512]{3,0,2,1:T(8,128)(2,1)}, bf16[32,4,1,512]{3,0,2,1:T(8,128)(2,1)S(1)}, u32[]{:S(2)}, u32[]{:S(2)}) collective-permute-start(bf16[32,4,1,512]{3,0,2,1:T(8,128)(2,1)} %convert_element_type.94), channel_id=1, source_target_pairs={{0,1},{1,2},{2,3},{3,4},{4,5},{5,6},{6,7},{7,8},{8,9},{9,10},{10,1... | collective-permute-start | bytes 393224 | tf_op jit(solution)/shard_map/ppermute | solution.py:24
  287.0 3.5 copy-start.3
  290.5 1.9 copy-start.5
  292.5 5.3 %collective-permute-start.1 = (bf16[32,4,1,512]{3,0,2,1:T(8,128)(2,1)S(1)}, bf16[32,4,1,512]{3,0,2,1:T(8,128)(2,1)S(1)}, u32[]{:S(2)}, u32[]{:S(2)}) collective-permute-start(bf16[32,4,1,512]{3,0,2,1:T(8,128)(2,1)S(1)} %slice.198), channel_id=1, source_target_pairs={{1,0},{2,1},{3,2},{4,3},{5,4},{6,5},{7,6},{8,7},{9,8},{10,9},{11,1... | collective-permute-start | bytes 393224 | tf_op jit(solution)/shard_map/ppermute | solution.py:24
  294.4 2.2 copy-start.6
  296.6 2.1 slice-start
  302.4 10.4 %copy-start.4 = (bf16[4,8,64,512]{3,2,1,0:T(8,128)(2,1)S(1)}, bf16[4,8,64,512]{3,2,1,0:T(8,128)(2,1)}, u32[]{:S(2)}) copy-start(bf16[4,8,64,512]{3,2,1,0:T(8,128)(2,1)} %copy-done.3) | copy-start | bytes 6291460
  302.4 10.4 %collective-permute-start.2 = (bf16[32,4,1,512]{3,0,2,1:T(8,128)(2,1)S(1)}, bf16[32,4,1,512]{3,0,2,1:T(8,128)(2,1)S(1)}, u32[]{:S(2)}, u32[]{:S(2)}) collective-permute-start(bf16[32,4,1,512]{3,0,2,1:T(8,128)(2,1)S(1)} %slice.197), channel_id=1, source_target_pairs={{0,1},{1,2},{2,3},{3,4},{4,5},{5,6},{6,7},{7,8},{8,9},{9,10},{10,1... | collective-permute-start | bytes 393224 | tf_op jit(solution)/shard_map/ppermute | solution.py:24
  318.0 7.6 %collective-permute-start.3 = (bf16[32,4,1,512]{3,0,2,1:T(8,128)(2,1)S(1)}, bf16[32,4,1,512]{3,0,2,1:T(8,128)(2,1)S(1)}, u32[]{:S(2)}, u32[]{:S(2)}) collective-permute-start(bf16[32,4,1,512]{3,0,2,1:T(8,128)(2,1)S(1)} %slice.196), channel_id=1, source_target_pairs={{1,0},{2,1},{3,2},{4,3},{5,4},{6,5},{7,6},{8,7},{9,8},{10,9},{11,1... | collective-permute-start | bytes 393224 | tf_op jit(solution)/shard_map/ppermute | solution.py:24
  331.6 10.2 %collective-permute-start.4 = (bf16[32,4,1,512]{3,0,2,1:T(8,128)(2,1)S(1)}, bf16[32,4,1,512]{3,0,2,1:T(8,128)(2,1)S(1)}, u32[]{:S(2)}, u32[]{:S(2)}) collective-permute-start(bf16[32,4,1,512]{3,0,2,1:T(8,128)(2,1)S(1)} %slice.195), channel_id=1, source_target_pairs={{0,1},{1,2},{2,3},{3,4},{4,5},{5,6},{6,7},{7,8},{8,9},{9,10},{10,1... | collective-permute-start | bytes 393224 | tf_op jit(solution)/shard_map/ppermute | solution.py:24
  347.1 7.6 %collective-permute-start.5 = (bf16[32,4,1,512]{3,0,2,1:T(8,128)(2,1)S(1)}, bf16[32,4,1,512]{3,0,2,1:T(8,128)(2,1)S(1)}, u32[]{:S(2)}, u32[]{:S(2)}) collective-permute-start(bf16[32,4,1,512]{3,0,2,1:T(8,128)(2,1)S(1)} %slice.194), channel_id=1, source_target_pairs={{1,0},{2,1},{3,2},{4,3},{5,4},{6,5},{7,6},{8,7},{9,8},{10,9},{11,1... | collective-permute-start | bytes 393224 | tf_op jit(solution)/shard_map/ppermute | solution.py:24
  360.6 10.2 %collective-permute-start.6 = (bf16[32,4,1,512]{3,0,2,1:T(8,128)(2,1)S(1)}, bf16[32,4,1,512]{3,0,2,1:T(8,128)(2,1)S(1)}, u32[]{:S(2)}, u32[]{:S(2)}) collective-permute-start(bf16[32,4,1,512]{3,0,2,1:T(8,128)(2,1)S(1)} %slice.193), channel_id=1, source_target_pairs={{0,1},{1,2},{2,3},{3,4},{4,5},{5,6},{6,7},{7,8},{8,9},{9,10},{10,1... | collective-permute-start | bytes 393224 | tf_op jit(solution)/shard_map/ppermute | solution.py:24
  376.1 7.8 %collective-permute-start.7 = (bf16[32,4,1,512]{3,0,2,1:T(8,128)(2,1)S(1)}, bf16[32,4,1,512]{3,0,2,1:T(8,128)(2,1)S(1)}, u32[]{:S(2)}, u32[]{:S(2)}) collective-permute-start(bf16[32,4,1,512]{3,0,2,1:T(8,128)(2,1)S(1)} %slice.192), channel_id=1, source_target_pairs={{1,0},{2,1},{3,2},{4,3},{5,4},{6,5},{7,6},{8,7},{9,8},{10,9},{11,1... | collective-permute-start | bytes 393224 | tf_op jit(solution)/shard_map/ppermute | solution.py:24
  389.8 10.2 %collective-permute-start.8 = (bf16[32,4,1,512]{3,0,2,1:T(8,128)(2,1)S(1)}, bf16[32,4,1,512]{3,0,2,1:T(8,128)(2,1)S(1)}, u32[]{:S(2)}, u32[]{:S(2)}) collective-permute-start(bf16[32,4,1,512]{3,0,2,1:T(8,128)(2,1)S(1)} %slice.191), channel_id=1, source_target_pairs={{0,1},{1,2},{2,3},{3,4},{4,5},{5,6},{6,7},{7,8},{8,9},{9,10},{10,1... | collective-permute-start | bytes 393224 | tf_op jit(solution)/shard_map/ppermute | solution.py:24
  405.4 7.6 %collective-permute-start.9 = (bf16[32,4,1,512]{3,0,2,1:T(8,128)(2,1)S(1)}, bf16[32,4,1,512]{3,0,2,1:T(8,128)(2,1)S(1)}, u32[]{:S(2)}, u32[]{:S(2)}) collective-permute-start(bf16[32,4,1,512]{3,0,2,1:T(8,128)(2,1)S(1)} %slice.190), channel_id=1, source_target_pairs={{1,0},{2,1},{3,2},{4,3},{5,4},{6,5},{7,6},{8,7},{9,8},{10,9},{11,1... | collective-permute-start | bytes 393224 | tf_op jit(solution)/shard_map/ppermute | solution.py:24
  418.9 8.4 %collective-permute-start.10 = (bf16[32,4,1,512]{3,0,2,1:T(8,128)(2,1)S(1)}, bf16[32,4,1,512]{3,0,2,1:T(8,128)(2,1)S(1)}, u32[]{:S(2)}, u32[]{:S(2)}) collective-permute-start(bf16[32,4,1,512]{3,0,2,1:T(8,128)(2,1)S(1)} %slice.189), channel_id=1, source_target_pairs={{0,1},{1,2},{2,3},{3,4},{4,5},{5,6},{6,7},{7,8},{8,9},{9,10},{10,1... | collective-permute-start | bytes 393224 | tf_op jit(solution)/shard_map/ppermute | solution.py:24
  427.3 7.6 %copy-start.1 = (f32[128,64]{0,1:T(8,128)S(1)}, f32[128,64]{0,1:T(8,128)}, u32[]{:S(2)}) copy-start(f32[128,64]{0,1:T(8,128)} %param.11) | copy-start | bytes 98308
Sparse Core Ops, SparseCore 0:
  15.0 85.3 all-gather.1
where the time goes:
time: 448 us; the launch traced here: 442 us
  blocking collectives  122 us (27%)
  waiting for transfers between devices  116 us (26%)
  other arithmetic  110 us (25%)
  local copies, waits for them, and re-layouts  39.3 us (9%)
  starting transfers between devices  24.5 us (5%)
  between operations  15 us (3%)
  matrix products  14.7 us (3%)
    psum x1, blocking collectives, local(): summed = lax.psum(block, 'pix')  110 us
    all_gather x1, waiting for transfers between devices, local(): everyone = lax.all_gather(flat, 'frame', axis=0, tiled=True)  82.8 us
    ppermute x11, waiting for transfers between devices, from_behind(): lax.ppermute(value, axis, [(source, source + steps) for source in range(l...  33 us
    div x5, other arithmetic, dual_update(): return ((first - step * down) / scale, (second - step * across) / scale)  27.1 us
    another operation x12, other arithmetic, mixing_matrix(): factor = jnp.linalg.cholesky(exact_dot(basis.T, image))  26.1 us
    ppermute x11, starting transfers between devices, from_behind(): lax.ppermute(value, axis, [(source, source + steps) for source in range(l...  24.5 us
    sub x5, other arithmetic, local(): smooth = source - lam * divergence(first, second)  24.3 us
    another operation x6, other arithmetic, mixing_matrix(): lax.linalg.triangular_solve(factor, image, left_side=False, lower=True, t...  16.6 us
  transfers between devices with their start and end apart: 12, of which 6 were waited for; matrix products, arithmetic and copies ran while one was open for 21% of the time, Pallas kernels for 0%

commit v1 on v0

v1 whole, which is shorter than its diff:
```python
import functools

import jax
import jax.numpy as jnp
from jax import lax
from jax.experimental import pallas as pl
from jax.experimental.pallas import tpu as pltpu
from jax.sharding import PartitionSpec as P

POWER = 3
NSWEEP = 5
STEP_SIZE = 0.125
MESH = pl.DeviceIdType.MESH
VMEM = pltpu.VMEM
SIDE = 4
BF16 = jnp.bfloat16
F32 = jnp.float32


def in_vmem(count):
    return [pl.BlockSpec(memory_space=pltpu.VMEM)] * count


def wrap(value, size):
    return lax.rem(value + size, size)


def place():
    x = lax.axis_index("frame")
    strip = lax.axis_index("pix")
    return x, strip, lax.div(strip, 8), lax.rem(lax.div(strip, 2), 4), lax.rem(strip, 2)


def greet(partners):
    barrier = pltpu.get_barrier_semaphore()
    for partner in partners:
        pl.semaphore_signal(barrier, inc=1, device_id=partner, device_id_type=MESH)
    pl.semaphore_wait(barrier, len(partners))


def swap_along_x(x, strip, src, dst, relay, local_sem, send_sem, recv_sem):
    right, left, opposite = wrap(x + 1, SIDE), wrap(x - 1, SIDE), wrap(x + 2, SIDE)
    half = src.shape[-1] // 2
    low, high = pl.ds(0, half), pl.ds(half, half)

    def copy(source, target, slot, to):
        return pltpu.make_async_remote_copy(
            src_ref=source,
            dst_ref=target,
            send_sem=send_sem.at[slot],
            recv_sem=recv_sem.at[slot],
            device_id=(to, strip),
            device_id_type=MESH,
        )

    out_low = copy(src.at[opposite, :, low], relay.at[0], 0, right)
    out_high = copy(src.at[opposite, :, high], relay.at[1], 1, left)
    to_right = copy(src.at[right], dst.at[x], 2, right)
    to_left = copy(src.at[left], dst.at[x], 3, left)
    out_low.start()
    out_high.start()
    to_right.start()
    to_left.start()
    mine = pltpu.make_async_copy(src.at[x], dst.at[x], local_sem)
    mine.start()
    out_low.wait_recv()
    on_low = copy(relay.at[0], dst.at[left, :, low], 4, right)
    on_low.start()
    out_high.wait_recv()
    on_high = copy(relay.at[1], dst.at[right, :, high], 5, left)
    on_high.start()
    mine.wait()
    copy(src.at[right], dst.at[left], 2, right).wait_recv()
    copy(src.at[left], dst.at[right], 3, left).wait_recv()
    copy(relay.at[0], dst.at[opposite, :, low], 4, right).wait_recv()
    copy(relay.at[1], dst.at[opposite, :, high], 5, left).wait_recv()
    for sent in (out_low, out_high, to_right, to_left, on_low, on_high):
        sent.wait_send()


def gram_kernel(
    resid, swapped, gram, relay, part, pieces, in_y, in_z, total,
    local_sem, swap_send, swap_recv, first_send, first_recv, y_send, y_recv, z_send, z_recv,
    last_send, last_recv,
):
    x, strip, y, z, core = place()
    group = x * 2 + core

    def of_group(k):
        return (lax.div(k, 2), strip - core + lax.rem(k, 2))

    def of_y(k):
        return (x, (k * 4 + z) * 2 + core)

    def of_z(k):
        return (x, (y * 4 + k) * 2 + core)

    partners = [of_group(wrap(group + k, 8)) for k in range(1, 8)]
    partners += [of_y(wrap(y + k, 4)) for k in range(1, 4)]
    partners += [of_z(wrap(z + k, 4)) for k in range(1, 4)]
    greet(partners)
    swap_along_x(x, strip, resid, swapped, relay, local_sem, swap_send, swap_recv)

    frames = part.shape[0] * part.shape[1]
    pixels = swapped.shape[-1]
    chunk = 1024

    def add(step, so_far):
        cols = pl.ds(pl.multiple_of(step * chunk, chunk), chunk)
        block = swapped[:, :, cols].reshape(frames, chunk)
        return so_far + lax.dot_general(
            block, block, (((1,), (1,)), ((), ())), preferred_element_type=F32
        )

    partial = lax.fori_loop(0, pixels // chunk, add, jnp.zeros((frames, frames), F32))
    part[...] = partial.reshape(part.shape)

    def exchange(index, size, where, source_of, buffer, send_sem, recv_sem):
        copies = []
        for k in range(1, size):
            to = wrap(index + k, size)
            copies.append(
                pltpu.make_async_remote_copy(
                    src_ref=source_of(to),
                    dst_ref=buffer.at[index],
                    send_sem=send_sem.at[k],
                    recv_sem=recv_sem.at[k],
                    device_id=where(to),
                    device_id_type=MESH,
                )
            )
        for copy in copies:
            copy.start()
        return copies

    def arrive(index, size, where, source_of, buffer, send_sem, recv_sem, copies):
        for k in range(1, size):
            pltpu.make_async_remote_copy(
                src_ref=source_of(wrap(index + k, size)),
                dst_ref=buffer.at[wrap(index - k, size)],
                send_sem=send_sem.at[k],
                recv_sem=recv_sem.at[k],
                device_id=where(wrap(index + k, size)),
                device_id_type=MESH,
            ).wait_recv()
        for copy in copies:
            copy.wait_send()

    def added(buffer, size):
        out = buffer[0]
        for k in range(1, size):
            out = out + buffer[k]
        return out

    args = (group, 8, of_group, lambda k: part.at[k], pieces, first_send, first_recv)
    copies = exchange(*args)
    pieces[group] = part[group]
    arrive(*args, copies)
    in_y[y] = added(pieces, 8)

    args = (y, 4, of_y, lambda k: in_y.at[y], in_y, y_send, y_recv)
    arrive(*args, exchange(*args))
    in_z[z] = added(in_y, 4)

    args = (z, 4, of_z, lambda k: in_z.at[z], in_z, z_send, z_recv)
    arrive(*args, exchange(*args))
    total[group] = added(in_z, 4)

    args = (group, 8, of_group, lambda k: total.at[group], total, last_send, last_recv)
    arrive(*args, exchange(*args))
    gram[...] = total[...].reshape(gram.shape)


def gram_of(resid):
    chans, count, pixels = resid.shape
    frames = count * SIDE
    rows = frames // 8
    dma = pltpu.SemaphoreType.DMA
    return pl.pallas_call(
        gram_kernel,
        out_shape=(
            jax.ShapeDtypeStruct((SIDE, count, pixels), BF16),
            jax.ShapeDtypeStruct((frames, frames), F32),
        ),
        in_specs=in_vmem(1),
        out_specs=tuple(in_vmem(2)),
        scratch_shapes=[
            VMEM((2, count, pixels // 2), BF16),
            VMEM((8, rows, frames), F32),
            VMEM((8, rows, frames), F32),
            VMEM((4, rows, frames), F32),
            VMEM((4, rows, frames), F32),
            VMEM((8, rows, frames), F32),
            dma,
            dma((6,)), dma((6,)),
            dma((8,)), dma((8,)),
            dma((4,)), dma((4,)),
            dma((4,)), dma((4,)),
            dma((8,)), dma((8,)),
        ],
        compiler_params=pltpu.CompilerParams(
            collective_id=0, has_side_effects=True, vmem_limit_bytes=40 << 20
        ),
        name="gram",
    )(resid)


def exact(left, right, dims):
    return lax.dot_general(
        left, right, (dims, ((), ())), precision=lax.Precision.HIGHEST, preferred_element_type=F32
    )


def lower_solve(square, sides):
    size = square.shape[0]
    blocks = size // 8
    sub = lax.broadcasted_iota(jnp.int32, (8, 128), 0)
    tiles = [square[8 * i : 8 * i + 8, :] for i in range(blocks)]
    hands = [[side[8 * i : 8 * i + 8, :] for i in range(blocks)] for side in sides]
    solved = [[] for _ in sides]
    for b in range(blocks):
        cols = [
            [
                jnp.broadcast_to(tiles[i][:, 8 * b + t : 8 * b + t + 1], (8, 128))
                if i >= b
                else None
                for i in range(blocks)
            ]
            for t in range(8)
        ]
        pivot = [
            [
                jnp.broadcast_to(cols[t][b][u : u + 1, :], (8, 128)) if u >= t else None
                for u in range(8)
            ]
            for t in range(8)
        ]
        rate = []
        low = [[None] * 8 for _ in range(8)]
        for t in range(8):
            rate.append(lax.rsqrt(pivot[t][t]))
            for u in range(t + 1, 8):
                low[u][t] = pivot[t][u] * rate[t]
            for u in range(t + 1, 8):
                for v in range(u, 8):
                    pivot[u][v] = pivot[u][v] - low[u][t] * low[v][t]

        def reduced(rows):
            done = []
            for t in range(8):
                value = rows[t]
                for s in range(t):
                    value = value - done[s] * low[t][s][:, : value.shape[1]]
                done.append(value * rate[t][:, : value.shape[1]])
            return done

        below = {i: reduced([cols[t][i] for t in range(8)]) for i in range(b + 1, blocks)}
        if b + 1 < blocks:
            across = reduced(
                [jnp.broadcast_to(tiles[b][t : t + 1, :], (8, size)) for t in range(8)]
            )
            for i in range(b + 1, blocks):
                for t in range(8):
                    tiles[i] = tiles[i] - below[i][t][:, :size] * across[t]
        for hand, out in zip(hands, solved):
            rows = reduced([jnp.broadcast_to(hand[b][t : t + 1, :], (8, 128)) for t in range(8)])
            tile = rows[0]
            for t in range(1, 8):
                tile = jnp.where(sub == t, rows[t], tile)
            out.append(tile)
            for i in range(b + 1, blocks):
                for t in range(8):
                    hand[i] = hand[i] - below[i][t] * rows[t]
    return [jnp.concatenate(out, axis=0) for out in solved]


def mixing_kernel(nval, gram_ref, sketch_ref, mixing_ref, gram_sc, basis_sc):
    gram_sc[...] = gram_ref[...] * (1.0 / nval)
    basis_sc[...] = sketch_ref[...]

    def turn(step, carry):
        basis = basis_sc[...]
        image = exact(basis, gram_sc[...], ((1,), (1,)))
        square = exact(basis, image, ((1,), (1,)))
        basis_sc[...] = lower_solve(square, [image])[0]
        return carry

    lax.fori_loop(0, POWER, turn, 0)
    basis = basis_sc[...]
    image = exact(basis, gram_sc[...], ((1,), (0,)))
    square = exact(basis, image, ((1,), (1,)))
    left, right = lower_solve(square, [basis, image])
    mixing_ref[...] = exact(right, left, ((0,), (0,))).astype(BF16)


def mixing_of(gram, sketch, nval):
    frames, rank = sketch.shape
    return pl.pallas_call(
        functools.partial(mixing_kernel, nval),
        out_shape=jax.ShapeDtypeStruct((frames, frames), BF16),
        in_specs=in_vmem(2),
        out_specs=in_vmem(1)[0],
        scratch_shapes=[VMEM((frames, frames), F32), VMEM((rank, frames), F32)],
        name="mixing",
    )(gram, sketch.T)


def back_kernel(
    swapped, weights, frames, valid, back, above, below,
    made, relay, top, bottom, local_sem, swap_send, swap_recv, halo_send, halo_recv,
):
    x, strip, _, _, _ = place()
    strips = lax.axis_size("pix")
    up, down = wrap(strip - 1, strips), wrap(strip + 1, strips)
    greet([(wrap(x + 1, SIDE), strip), (wrap(x - 1, SIDE), strip), (x, up), (x, down)])
    side, count, pixels = swapped.shape
    chunk = 1024
    mix = weights[...]

    def multiply(step, carry):
        cols = pl.ds(pl.multiple_of(step * chunk, chunk), chunk)
        block = swapped[:, :, cols].reshape(side * count, chunk)
        out = jnp.dot(mix, block, preferred_element_type=F32)
        made[:, :, cols] = out.astype(BF16).reshape(side, count, chunk)
        return carry

    lax.fori_loop(0, pixels // chunk, multiply, 0)
    swap_along_x(x, strip, made, back, relay, local_sem, swap_send, swap_recv)
    width = top.shape[-1]
    for chan in range(side):
        for target, start in ((top, 0), (bottom, pixels - width)):
            cols = slice(start, start + width)
            source = frames[chan, :, cols].astype(F32) - back[chan, :, cols].astype(F32)
            if chan == side - 1:
                source = source * valid[:, cols].astype(F32)
            target[chan] = source.astype(BF16)
    copies = []
    for k, (source, target, to) in enumerate(((top, below, up), (bottom, above, down))):
        copies.append(
            pltpu.make_async_remote_copy(
                src_ref=source,
                dst_ref=target,
                send_sem=halo_send.at[k],
                recv_sem=halo_recv.at[k],
                device_id=(x, to),
                device_id_type=MESH,
            )
        )
    for copy in copies:
        copy.start()
    for copy in copies:
        copy.wait()


def back_of(swapped, weights, frames, valid, cols):
    side, count, pixels = swapped.shape
    dma = pltpu.SemaphoreType.DMA
    halo = (side, count, NSWEEP * cols)
    return pl.pallas_call(
        back_kernel,
        out_shape=(
            jax.ShapeDtypeStruct(swapped.shape, BF16),
            jax.ShapeDtypeStruct(halo, BF16),
            jax.ShapeDtypeStruct(halo, BF16),
        ),
        in_specs=in_vmem(4),
        out_specs=tuple(in_vmem(3)),
        scratch_shapes=[
            VMEM(swapped.shape, BF16),
            VMEM((2, count, pixels // 2), BF16),
            VMEM(halo, BF16),
            VMEM(halo, BF16),
            dma,
            dma((6,)), dma((6,)),
            dma((2,)), dma((2,)),
        ],
        compiler_params=pltpu.CompilerParams(
            collective_id=1, has_side_effects=True, vmem_limit_bytes=40 << 20
        ),
        name="back",
    )(swapped, weights, frames, valid)


def tv_kernel(
    strips, strip_ref, lam_ref, frames, back, valid, above, below, out, source, first, second
):
    chan = pl.program_id(0)
    last = pl.num_programs(0) - 1
    lam = lam_ref[chan]
    step = STEP_SIZE / lam
    strip = strip_ref[0]
    halo = NSWEEP
    span, lines, cols = source.shape
    rows = span - 2 * halo
    height = strips * rows

    for r in range(halo):
        source[r] = above[0, :, r * cols : (r + 1) * cols].astype(F32)
        source[halo + rows + r] = below[0, :, r * cols : (r + 1) * cols].astype(F32)
    for r in range(rows):
        where = slice(r * cols, (r + 1) * cols)
        ok = jnp.where(chan == last, valid[:, where].astype(F32), 1.0)
        source[halo + r] = (
            frames[0, :, where].astype(F32) - back[0, :, where].astype(F32)
        ) * ok

    inner_col = (
        lax.broadcasted_iota(jnp.int32, (lines, cols), 1) < cols - 1
    )

    def update(r, smooth, after, old_first, old_second):
        row = strip * rows + r - halo
        inside = jnp.where((row >= 0) & (row < height - 1), F32(1.0), F32(0.0))
        down = (after - smooth) * inside
        across = jnp.where(inner_col, pltpu.roll(smooth, cols - 1, 1) - smooth, 0.0)
        square = down * down + across * across
        size = square * lax.rsqrt(jnp.maximum(square, 1e-37))
        rate = 1.0 / (1.0 + step * size)
        new_first = -step * down if old_first is None else old_first - step * down
        new_second = -step * across if old_second is None else old_second - step * across
        first[r] = new_first * rate
        second[r] = new_second * rate

    def start(r, smooth):
        after = source[r + 1]
        update(r, smooth, after, None, None)
        return after

    lax.fori_loop(0, span - 1, start, source[0])

    def image(r, up, here, beside):
        turn = here - up + (beside - pltpu.roll(beside, 1, 1))
        return source[r] - lam * turn

    def line(r, carry):
        smooth, here, beside = carry
        next_first, next_second = first[r + 1], second[r + 1]
        after = image(r + 1, here, next_first, next_second)
        update(r, smooth, after, here, beside)
        return after, next_first, next_second

    for sweep in range(1, NSWEEP):
        here, beside = first[sweep], second[sweep]
        smooth = image(sweep, first[sweep - 1], here, beside)
        lax.fori_loop(sweep, span - 1 - sweep, line, (smooth, here, beside))
    for r in range(rows):
        value = image(halo + r, first[halo + r - 1], first[halo + r], second[halo + r])
        out[0, :, r * cols : (r + 1) * cols] = value.astype(BF16)


def foreground_of(frames, back, valid, above, below, lam, strip, strips, cols):
    chans, count, pixels = frames.shape
    lines = 16
    rows = pixels // cols
    span = rows + 2 * NSWEEP
    whole = pl.BlockSpec((1, lines, pixels), lambda c, f, *_: (c, f, 0))
    edge = pl.BlockSpec((1, lines, NSWEEP * cols), lambda c, f, *_: (c, f, 0))
    scalar = pl.BlockSpec(memory_space=pltpu.SMEM)
    return pl.pallas_call(
        functools.partial(tv_kernel, strips),
        grid=(chans, count // lines),
        out_shape=jax.ShapeDtypeStruct(frames.shape, BF16),
        in_specs=[
            scalar,
            scalar,
            whole,
            whole,
            pl.BlockSpec((lines, pixels), lambda c, f: (f, 0)),
            edge,
            edge,
        ],
        out_specs=whole,
        scratch_shapes=[VMEM((span, lines, cols), F32)] * 3,
        compiler_params=pltpu.CompilerParams(vmem_limit_bytes=40 << 20),
        name="tv",
    )(strip, lam, frames, back, valid, above, below)


def local(frames, prev_fg, depth_valid, sketch, tv_weight):
    count, chans, rows, cols = frames.shape
    strips = lax.axis_size("pix")
    nval = chans * rows * strips * cols
    chan_ids = lax.broadcasted_iota(jnp.int32, (1, chans, 1, 1), 1)
    depth_ok = depth_valid[:, None, :, :].astype(F32)
    valid = jnp.where(chan_ids == chans - 1, depth_ok, F32(1.0))
    resid = ((frames.astype(F32) - prev_fg.astype(F32)) * valid).astype(BF16)

    def flat(value):
        return value.transpose(1, 0, 2, 3).reshape(chans, count, rows * cols)

    resid, frames = flat(resid), flat(frames)
    ok = depth_valid.astype(BF16).reshape(count, rows * cols)
    swapped, gram = gram_of(resid)
    weights = mixing_of(gram, sketch, nval)
    back, above, below = back_of(swapped, weights, frames, ok, cols)
    strip = lax.axis_index("pix").reshape(1)
    fore = foreground_of(frames, back, ok, above, below, tv_weight, strip, strips, cols)

    def unflat(value):
        return value.reshape(chans, count, rows, cols).transpose(1, 0, 2, 3)

    return unflat(back), unflat(fore)


def solution(mesh):
    placed = (
        P("frame", None, "pix", None),
        P("frame", None, "pix", None),
        P("frame", "pix", None),
        P(),
        P(),
    )
    return jax.shard_map(
        local,
        mesh=mesh,
        in_specs=placed,
        out_specs=(P("frame", None, "pix", None), P("frame", None, "pix", None)),
        check_vma=False,
    )
```

time: 448 us -> 216 us (0.48)
  the two profiles are of different devices: /device:TPU:8 before, /device:TPU:6 now
where the time goes in v1:
time: 216 us; the launch traced here: 214 us
  Pallas kernels  190 us (88%)
  local copies, waits for them, and re-layouts  16.8 us (8%)
  other arithmetic  6.23 us (3%)
    pallas_call x1, Pallas kernels, foreground_of(): pl.pallas_call(functools.partial(tv_kernel, strips), grid=(chans, count /...  93.7 us
    pallas_call x1, Pallas kernels, gram_of(): pl.pallas_call(gram_kernel, out_shape=(jax.ShapeDtypeStruct((SIDE, count,...  47 us
    pallas_call x1, Pallas kernels, back_of(): pl.pallas_call(back_kernel, out_shape=(jax.ShapeDtypeStruct(swapped.shape...  38.5 us
    reshape x4, local copies, waits for them, and re-layouts, flat(): return value.transpose(1, 0, 2, 3).reshape(chans, count, rows * cols)  11.7 us
    pallas_call x1, Pallas kernels, mixing_of(): pl.pallas_call(functools.partial(mixing_kernel, nval), out_shape=jax.Shap...  11.1 us

profile of v1, /device:TPU:6, one launch (start us, length us, event | category | flops | bytes accessed | tf_op | source)
XLA Modules:
  0.0 214.0 jit_solution(2681038826576191699)
XLA Ops:
  0.6 0.0 copy-start.3
  0.7 2.1 fusion.1
  2.8 0.3 copy.13
  3.1 0.0 copy-done.3
  3.1 4.1 %fusion = bf16[4,32,16,512]{3,2,0,1:T(8,128)(2,1)} fusion(bf16[32,4,16,512]{3,2,1,0:T(8,128)(2,1)} %param.6, bf16[32,4,16,512]{3,2,1,0:T(8,128)(2,1)S(1)} %copy-done.3, f32[32,16,512]{2,1,0:T(8,128)S(1)} %get-tuple-element.13, pred[4]{0:T(512)(128)(4,1)S(1)} %iota_compare_fusion), kind=kLoop, calls=%fused_computation.1 | loop fusion | flops 6291456 | bytes 7340036 | tf_op jit(solution)/shard_map/transpose | solution.py:489
  7.2 3.3 %reshape.35 = bf16[4,32,8192]{2,0,1:T(4,128)(2,1)S(1)} reshape(bf16[4,32,16,512]{3,2,0,1:T(8,128)(2,1)} %fusion) | data formatting | bytes 4194304 | tf_op jit(solution)/shard_map/reshape | solution.py:489
  10.5 1.2 copy.11.resid
  11.7 47.0 %gram.1 = (bf16[4,32,8192]{2,1,0:T(8,128)(2,1)S(1)}, f32[128,128]{1,0:T(8,128)S(1)}) custom-call(bf16[4,32,8192]{2,1,0:T(8,128)(2,1)S(1)} %copy.11.resid), custom_call_target="tpu_custom_call" | custom-call | tf_op jit(solution)/shard_map/gram/pallas_call | solution.py:179
  58.7 0.0 copy-start.1
  58.7 0.6 copy-done.1
  59.3 11.1 %mixing.1.weights = bf16[128,128]{1,0:T(8,128)(2,1)} custom-call(f32[128,128]{1,0:T(8,128)} %copy-done.1, f32[64,128]{1,0:T(8,128)} %bitcast.43), custom_call_target="tpu_custom_call" | custom-call | tf_op jit(solution)/shard_map/mixing/pallas_call | solution.py:298
  70.4 4.5 %reshape.36 = bf16[4,32,8192]{2,0,1:T(4,128)(2,1)} reshape(bf16[4,32,16,512]{3,2,0,1:T(8,128)(2,1)} %bitcast.39) | data formatting | bytes 4194304 | tf_op jit(solution)/shard_map/reshape | solution.py:489
  74.9 0.0 copy-start
  74.9 2.7 %copy.12.frames = bf16[4,32,8192]{2,1,0:T(8,128)(2,1)S(1)} copy(bf16[4,32,8192]{2,0,1:T(4,128)(2,1)} %reshape.36) | data formatting | bytes 4194304 | tf_op jit(solution)/shard_map/reshape | solution.py:489
  77.6 0.0 copy-done
  77.6 0.0 copy-start.2
  77.6 38.5 %back.1 = (bf16[4,32,8192]{2,1,0:T(8,128)(2,1)S(1)}, bf16[4,32,2560]{2,1,0:T(8,128)(2,1)S(1)}, bf16[4,32,2560]{2,1,0:T(8,128)(2,1)S(1)}) custom-call(bf16[4,32,8192]{2,1,0:T(8,128)(2,1)S(1)} %get-tuple-element.7.swapped, bf16[128,128]{1,0:T(8,128)(2,1)S(1)} %copy-done, bf16[4,32,8192]{2,1,0:T(8,128)(2,1)S(1)} %copy.12.frames, bf16[32,8192]{1,0:T(8,128)(2,1)S(1)} %bitcast.37), custom_call_target="tpu_custom_call" | custom-call | tf_op jit(solution)/shard_map/back/pallas_call | solution.py:359
  116.2 0.0 copy-done.2
  116.2 93.7 %tv.1 = bf16[4,32,8192]{2,1,0:T(8,128)(2,1)S(1)} custom-call(s32[1]{0:T(128)} %bitcast.4.strip_ref, f32[4]{0:T(128)S(1)} %copy-done.2, bf16[4,32,8192]{2,1,0:T(8,128)(2,1)S(1)} %copy.12.frames, bf16[4,32,8192]{2,1,0:T(8,128)(2,1)S(1)} %get-tuple-element.9.back, bf16[32,8192]{1,0:T(8,128)(2,1)S(1)} %bitcast.38, ...), custom_call_target="tpu_custom_call" | custom-call | tf_op jit(solution)/shard_map/tv/pallas_call | solution.py:459
  209.9 0.9 copy.15
  210.7 0.8 copy.14
  211.6 2.5 %copy_bitcast_fusion = (bf16[32,4,16,512]{3,2,1,0:T(8,128)(2,1)}, bf16[32,4,16,512]{3,2,1,0:T(8,128)(2,1)}) fusion(bf16[4,32,16,512]{3,2,1,0:T(8,128)(2,1)S(1)} %bitcast.41, bf16[4,32,16,512]{3,2,1,0:T(8,128)(2,1)S(1)} %bitcast.40), kind=kLoop, calls=%fused_computation.2 | loop fusion | bytes 8388608 | tf_op jit(solution)/shard_map/transpose | solution.py:500
  (1 shorter events, 0.0 us)
Async XLA Ops:
  0.6 2.4 %copy-start.3 = (bf16[32,4,16,512]{3,2,1,0:T(8,128)(2,1)S(1)}, bf16[32,4,16,512]{3,2,1,0:T(8,128)(2,1)}, u32[]{:S(2)}) copy-start(bf16[32,4,16,512]{3,2,1,0:T(8,128)(2,1)} %param.5) | copy-start | bytes 6291460
  58.7 0.6 copy-start.1
  74.9 2.8 %copy-start = (bf16[128,128]{1,0:T(8,128)(2,1)S(1)}, bf16[128,128]{1,0:T(8,128)(2,1)}, u32[]{:S(2)}) copy-start(bf16[128,128]{1,0:T(8,128)(2,1)} %mixing.1.weights) | copy-start | bytes 98308
  77.6 38.6 %copy-start.2 = (f32[4]{0:T(128)S(1)}, f32[4]{0:T(128)}, u32[]{:S(2)}) copy-start(f32[4]{0:T(128)} %lam_ref.1) | copy-start | bytes 52

commit v2 on v1

--- a/solution.py
+++ b/solution.py
@@ -381,76 +381,88 @@
     )(swapped, weights, frames, valid)
 
 
-def tv_kernel(
-    strips, strip_ref, lam_ref, frames, back, valid, above, below, out, source, first, second
-):
+def tv_kernel(strips, strip_ref, lam_ref, frames, back, valid, above, below, out, source, first, second):
     chan = pl.program_id(0)
     last = pl.num_programs(0) - 1
     lam = lam_ref[chan]
-    step = STEP_SIZE / lam
+    inverse = 1.0 / lam
     strip = strip_ref[0]
     halo = NSWEEP
     span, lines, cols = source.shape
     rows = span - 2 * halo
-    height = strips * rows
+    tiles = cols // 128
+    lane = lax.broadcasted_iota(jnp.int32, (lines, 128), 1)
+    open_above = jnp.where(strip > 0, F32(1.0), F32(0.0))
+    open_below = jnp.where(strip < strips - 1, F32(1.0), F32(0.0))
+
+    def tile(ref, r):
+        return [ref[r, :, 128 * j : 128 * j + 128] for j in range(tiles)]
+
+    def put(ref, r, values):
+        for j in range(tiles):
+            ref[r, :, 128 * j : 128 * j + 128] = values[j]
 
     for r in range(halo):
-        source[r] = above[0, :, r * cols : (r + 1) * cols].astype(F32)
-        source[halo + rows + r] = below[0, :, r * cols : (r + 1) * cols].astype(F32)
+        source[r] = above[0, :, r * cols : (r + 1) * cols].astype(F32) * 0.125
+        source[halo + rows + r] = below[0, :, r * cols : (r + 1) * cols].astype(F32) * 0.125
     for r in range(rows):
         where = slice(r * cols, (r + 1) * cols)
         ok = jnp.where(chan == last, valid[:, where].astype(F32), 1.0)
-        source[halo + r] = (
-            frames[0, :, where].astype(F32) - back[0, :, where].astype(F32)
-        ) * ok
-
-    inner_col = (
-        lax.broadcasted_iota(jnp.int32, (lines, cols), 1) < cols - 1
-    )
-
-    def update(r, smooth, after, old_first, old_second):
-        row = strip * rows + r - halo
-        inside = jnp.where((row >= 0) & (row < height - 1), F32(1.0), F32(0.0))
-        down = (after - smooth) * inside
-        across = jnp.where(inner_col, pltpu.roll(smooth, cols - 1, 1) - smooth, 0.0)
-        square = down * down + across * across
-        size = square * lax.rsqrt(jnp.maximum(square, 1e-37))
-        rate = 1.0 / (1.0 + step * size)
-        new_first = -step * down if old_first is None else old_first - step * down
-        new_second = -step * across if old_second is None else old_second - step * across
-        first[r] = new_first * rate
-        second[r] = new_second * rate
-
-    def start(r, smooth):
-        after = source[r + 1]
-        update(r, smooth, after, None, None)
-        return after
-
-    lax.fori_loop(0, span - 1, start, source[0])
-
-    def image(r, up, here, beside):
-        turn = here - up + (beside - pltpu.roll(beside, 1, 1))
-        return source[r] - lam * turn
-
-    def line(r, carry):
-        smooth, here, beside = carry
-        next_first, next_second = first[r + 1], second[r + 1]
-        after = image(r + 1, here, next_first, next_second)
-        update(r, smooth, after, here, beside)
-        return after, next_first, next_second
-
+        source[halo + r] = (frames[0, :, where].astype(F32) - back[0, :, where].astype(F32)) * (ok * 0.125)
+
+    def before(values):
+        turned = [pltpu.roll(v, 1, 1) for v in values]
+        return [jnp.where(lane == 0, turned[j - 1] if j else 0.0, turned[j]) for j in range(tiles)]
+
+    def after(values):
+        turned = [pltpu.roll(v, 127, 1) for v in values]
+        return [jnp.where(lane == 127, turned[j + 1] if j + 1 < tiles else values[j], turned[j]) for j in range(tiles)]
+
+    def image(r, up, here, beside, scale=0.125):
+        left = before(beside)
+        return [s - scale * ((h - u) + (b - l)) for s, u, h, b, l in zip(tile(source, r), up, here, beside, left)]
+
+    def update(r, smooth, under, here, beside):
+        right = after(smooth)
+        news = []
+        for j in range(tiles):
+            down = under[j] - smooth[j]
+            if r == halo - 1:
+                down = down * open_above
+            if r == halo + rows - 1:
+                down = down * open_below
+            across = right[j] - smooth[j]
+            square = jnp.maximum(down * down + across * across, 1e-37)
+            rate = 1.0 / (1.0 + inverse * (square * lax.rsqrt(square)))
+            a = -down if here is None else here[j] - down
+            b = -across if beside is None else beside[j] - across
+            news.append((a * rate, b * rate))
+        put(first, r, [n[0] for n in news])
+        put(second, r, [n[1] for n in news])
+
+    smooth = tile(source, 0)
+    for r in range(span - 1):
+        under = tile(source, r + 1)
+        update(r, smooth, under, None, None)
+        smooth = under
     for sweep in range(1, NSWEEP):
-        here, beside = first[sweep], second[sweep]
-        smooth = image(sweep, first[sweep - 1], here, beside)
-        lax.fori_loop(sweep, span - 1 - sweep, line, (smooth, here, beside))
+        here, beside = tile(first, sweep), tile(second, sweep)
+        smooth = image(sweep, tile(first, sweep - 1), here, beside)
+        for r in range(sweep, span - 1 - sweep):
+            next_here, next_beside = tile(first, r + 1), tile(second, r + 1)
+            under = image(r + 1, here, next_here, next_beside)
+            update(r, smooth, under, here, beside)
+            smooth, here, beside = under, next_here, next_beside
     for r in range(rows):
-        value = image(halo + r, first[halo + r - 1], first[halo + r], second[halo + r])
-        out[0, :, r * cols : (r + 1) * cols] = value.astype(BF16)
+        i = halo + r
+        values = image(i, tile(first, i - 1), tile(first, i), tile(second, i))
+        for j in range(tiles):
+            out[0, :, r * cols + 128 * j : r * cols + 128 * j + 128] = (values[j] * 8.0).astype(BF16)
 
 
 def foreground_of(frames, back, valid, above, below, lam, strip, strips, cols):
     chans, count, pixels = frames.shape
-    lines = 16
+    lines = 32
     rows = pixels // cols
     span = rows + 2 * NSWEEP
     whole = pl.BlockSpec((1, lines, pixels), lambda c, f, *_: (c, f, 0))

time: 216 us -> 149 us (0.69)
  Pallas kernels: 190 us -> 123 us
    pallas_call x1, Pallas kernels: 93.7 us -> 26.3 us  [foreground_of(): pl.pallas_call(functools.partial(tv_kernel, strips), grid=(chans, count /...]
where the time goes in v2:
time: 149 us; the launch traced here: 147 us
  Pallas kernels  123 us (83%)
  local copies, waits for them, and re-layouts  16.8 us (11%)
  other arithmetic  6.09 us (4%)
    pallas_call x1, Pallas kernels, gram_of(): pl.pallas_call(gram_kernel, out_shape=(jax.ShapeDtypeStruct((SIDE, count,...  47 us
    pallas_call x1, Pallas kernels, back_of(): pl.pallas_call(back_kernel, out_shape=(jax.ShapeDtypeStruct(swapped.shape...  38.5 us
    pallas_call x1, Pallas kernels, foreground_of(): pl.pallas_call(functools.partial(tv_kernel, strips), grid=(chans, count /...  26.3 us
    reshape x4, local copies, waits for them, and re-layouts, flat(): return value.transpose(1, 0, 2, 3).reshape(chans, count, rows * cols)  11.7 us
    pallas_call x1, Pallas kernels, mixing_of(): pl.pallas_call(functools.partial(mixing_kernel, nval), out_shape=jax.Shap...  11.1 us
    transpose x1, other arithmetic, flat(): return value.transpose(1, 0, 2, 3).reshape(chans, count, rows * cols)  4.14 us

profile of v2, /device:TPU:6, one launch (start us, length us, event | category | flops | bytes accessed | tf_op | source)
XLA Modules:
  0.0 146.5 jit_solution(17966003165512875305)
XLA Ops:
  0.6 0.0 copy-start.3
  0.7 1.9 %fusion.1 = (bf16[32,16,512]{2,1,0:T(8,128)(2,1)S(1)}, f32[32,16,512]{2,1,0:T(8,128)S(1)}) fusion(s32[32,16,512]{2,1,0:T(8,128)} %param.7), kind=kLoop, calls=%fused_computation.5 | loop fusion | flops 524288 | bytes 2621440 | tf_op jit(solution)/shard_map/convert_element_type | solution.py:504
  2.6 0.3 copy.13
  2.9 0.0 copy-done.3
  2.9 4.1 %fusion = bf16[4,32,16,512]{3,2,0,1:T(8,128)(2,1)} fusion(bf16[32,4,16,512]{3,2,1,0:T(8,128)(2,1)} %param.6, bf16[32,4,16,512]{3,2,1,0:T(8,128)(2,1)S(1)} %copy-done.3, f32[32,16,512]{2,1,0:T(8,128)S(1)} %get-tuple-element.13, pred[4]{0:T(512)(128)(4,1)S(1)} %iota_compare_fusion), kind=kLoop, calls=%fused_computation.1 | loop fusion | flops 6291456 | bytes 7340036 | tf_op jit(solution)/shard_map/transpose | solution.py:501
  7.1 3.3 %reshape.35 = bf16[4,32,8192]{2,0,1:T(4,128)(2,1)S(1)} reshape(bf16[4,32,16,512]{3,2,0,1:T(8,128)(2,1)} %fusion) | data formatting | bytes 4194304 | tf_op jit(solution)/shard_map/reshape | solution.py:501
  10.4 1.2 copy.11.resid
  11.5 47.0 %gram.1 = (bf16[4,32,8192]{2,1,0:T(8,128)(2,1)S(1)}, f32[128,128]{1,0:T(8,128)S(1)}) custom-call(bf16[4,32,8192]{2,1,0:T(8,128)(2,1)S(1)} %copy.11.resid), custom_call_target="tpu_custom_call" | custom-call | tf_op jit(solution)/shard_map/gram/pallas_call | solution.py:179
  58.5 0.0 copy-start.1
  58.5 0.6 copy-done.1
  59.2 11.1 %mixing.1.weights = bf16[128,128]{1,0:T(8,128)(2,1)} custom-call(f32[128,128]{1,0:T(8,128)} %copy-done.1, f32[64,128]{1,0:T(8,128)} %bitcast.43), custom_call_target="tpu_custom_call" | custom-call | tf_op jit(solution)/shard_map/mixing/pallas_call | solution.py:298
  70.2 4.5 %reshape.36 = bf16[4,32,8192]{2,0,1:T(4,128)(2,1)} reshape(bf16[4,32,16,512]{3,2,0,1:T(8,128)(2,1)} %bitcast.39) | data formatting | bytes 4194304 | tf_op jit(solution)/shard_map/reshape | solution.py:501
  74.7 0.0 copy-start
  74.7 2.7 %copy.12.frames = bf16[4,32,8192]{2,1,0:T(8,128)(2,1)S(1)} copy(bf16[4,32,8192]{2,0,1:T(4,128)(2,1)} %reshape.36) | data formatting | bytes 4194304 | tf_op jit(solution)/shard_map/reshape | solution.py:501
  77.5 0.0 copy-done
  77.5 0.0 copy-start.2
  77.5 38.5 %back.1 = (bf16[4,32,8192]{2,1,0:T(8,128)(2,1)S(1)}, bf16[4,32,2560]{2,1,0:T(8,128)(2,1)S(1)}, bf16[4,32,2560]{2,1,0:T(8,128)(2,1)S(1)}) custom-call(bf16[4,32,8192]{2,1,0:T(8,128)(2,1)S(1)} %get-tuple-element.7.swapped, bf16[128,128]{1,0:T(8,128)(2,1)S(1)} %copy-done, bf16[4,32,8192]{2,1,0:T(8,128)(2,1)S(1)} %copy.12.frames, bf16[32,8192]{1,0:T(8,128)(2,1)S(1)} %bitcast.37), custom_call_target="tpu_custom_call" | custom-call | tf_op jit(solution)/shard_map/back/pallas_call | solution.py:359
  116.1 0.0 copy-done.2
  116.1 26.3 %tv.1 = bf16[4,32,8192]{2,1,0:T(8,128)(2,1)S(1)} custom-call(s32[1]{0:T(128)} %bitcast.4.strip_ref, f32[4]{0:T(128)S(1)} %copy-done.2, bf16[4,32,8192]{2,1,0:T(8,128)(2,1)S(1)} %copy.12.frames, bf16[4,32,8192]{2,1,0:T(8,128)(2,1)S(1)} %get-tuple-element.9.back, bf16[32,8192]{1,0:T(8,128)(2,1)S(1)} %bitcast.38, ...), custom_call_target="tpu_custom_call" | custom-call | tf_op jit(solution)/shard_map/tv/pallas_call | solution.py:471
  142.4 0.9 copy.15
  143.2 0.8 copy.14
  144.1 2.5 %copy_bitcast_fusion = (bf16[32,4,16,512]{3,2,1,0:T(8,128)(2,1)}, bf16[32,4,16,512]{3,2,1,0:T(8,128)(2,1)}) fusion(bf16[4,32,16,512]{3,2,1,0:T(8,128)(2,1)S(1)} %bitcast.41, bf16[4,32,16,512]{3,2,1,0:T(8,128)(2,1)S(1)} %bitcast.40), kind=kLoop, calls=%fused_computation.2 | loop fusion | bytes 8388608 | tf_op jit(solution)/shard_map/transpose | solution.py:512
  (1 shorter events, 0.0 us)
Async XLA Ops:
  0.6 2.3 %copy-start.3 = (bf16[32,4,16,512]{3,2,1,0:T(8,128)(2,1)S(1)}, bf16[32,4,16,512]{3,2,1,0:T(8,128)(2,1)}, u32[]{:S(2)}) copy-start(bf16[32,4,16,512]{3,2,1,0:T(8,128)(2,1)} %param.5) | copy-start | bytes 6291460
  58.5 0.6 copy-start.1
  74.7 2.8 %copy-start = (bf16[128,128]{1,0:T(8,128)(2,1)S(1)}, bf16[128,128]{1,0:T(8,128)(2,1)}, u32[]{:S(2)}) copy-start(bf16[128,128]{1,0:T(8,128)(2,1)} %mixing.1.weights) | copy-start | bytes 98308
  77.5 38.6 %copy-start.2 = (f32[4]{0:T(128)S(1)}, f32[4]{0:T(128)}, u32[]{:S(2)}) copy-start(f32[4]{0:T(128)} %lam_ref.1) | copy-start | bytes 52

commit v3 on v2

--- a/solution.py
+++ b/solution.py
@@ -38,53 +38,70 @@
     pl.semaphore_wait(barrier, len(partners))
 
 
-def swap_along_x(x, strip, src, dst, relay, local_sem, send_sem, recv_sem):
-    right, left, opposite = wrap(x + 1, SIDE), wrap(x - 1, SIDE), wrap(x + 2, SIDE)
-    half = src.shape[-1] // 2
-    low, high = pl.ds(0, half), pl.ds(half, half)
-
-    def copy(source, target, slot, to):
-        return pltpu.make_async_remote_copy(
-            src_ref=source,
-            dst_ref=target,
-            send_sem=send_sem.at[slot],
-            recv_sem=recv_sem.at[slot],
-            device_id=(to, strip),
-            device_id_type=MESH,
-        )
-
-    out_low = copy(src.at[opposite, :, low], relay.at[0], 0, right)
-    out_high = copy(src.at[opposite, :, high], relay.at[1], 1, left)
-    to_right = copy(src.at[right], dst.at[x], 2, right)
-    to_left = copy(src.at[left], dst.at[x], 3, left)
-    out_low.start()
-    out_high.start()
-    to_right.start()
-    to_left.start()
-    mine = pltpu.make_async_copy(src.at[x], dst.at[x], local_sem)
-    mine.start()
-    out_low.wait_recv()
-    on_low = copy(relay.at[0], dst.at[left, :, low], 4, right)
-    on_low.start()
-    out_high.wait_recv()
-    on_high = copy(relay.at[1], dst.at[right, :, high], 5, left)
-    on_high.start()
-    mine.wait()
-    copy(src.at[right], dst.at[left], 2, right).wait_recv()
-    copy(src.at[left], dst.at[right], 3, left).wait_recv()
-    copy(relay.at[0], dst.at[opposite, :, low], 4, right).wait_recv()
-    copy(relay.at[1], dst.at[opposite, :, high], 5, left).wait_recv()
-    for sent in (out_low, out_high, to_right, to_left, on_low, on_high):
-        sent.wait_send()
+def send_along_x(x, strip, src, dst, send_sem, recv_sem, offset):
+    to = wrap(x + offset, SIDE)
+    return pltpu.make_async_remote_copy(
+        src_ref=src.at[to],
+        dst_ref=dst.at[x],
+        send_sem=send_sem.at[offset],
+        recv_sem=recv_sem.at[offset],
+        device_id=(to, strip),
+        device_id_type=MESH,
+    )
+
+
+def taken_along_x(x, strip, src, dst, send_sem, recv_sem, offset):
+    origin = wrap(x - offset, SIDE)
+    return pltpu.make_async_remote_copy(
+        src_ref=src.at[origin],
+        dst_ref=dst.at[origin],
+        send_sem=send_sem.at[offset],
+        recv_sem=recv_sem.at[offset],
+        device_id=(origin, strip),
+        device_id_type=MESH,
+    )
+
+
+ORDER = (2, 1, 3)
+
+
+def lay(lines, start, value):
+    count, rows, cols = value.shape
+    value = value.reshape(count * rows, cols)
+    for j in range(lines.shape[0]):
+        lines[j, start * rows : (start + count) * rows, :] = value[:, 128 * j : 128 * j + 128]
+
+
+def turned(lines, write, rows):
+    tiles, size, _ = lines.shape
+    for r in range(rows):
+        for j in range(tiles):
+            start = (r * tiles + j) * 128
+            value = lines.at[j][pl.ds(r, size // rows, stride=rows), :]
+            write(slice(start, start + 128), value)
 
 
 def gram_kernel(
-    resid, swapped, gram, relay, part, pieces, in_y, in_z, total,
-    local_sem, swap_send, swap_recv, first_send, first_recv, y_send, y_recv, z_send, z_recv,
+    frames_hbm, prev_hbm, depth_hbm, swapped, gram, flat_frames, flat_valid,
+    frames, prev, depth, flat, lines, part, pieces, in_y, in_z, total,
+    load_sem, swap_send, swap_recv, first_send, first_recv, y_send, y_recv, z_send, z_recv,
     last_send, last_recv,
 ):
     x, strip, y, z, core = place()
     group = x * 2 + core
+    count, chans, rows, cols = frames.shape
+    channels = [wrap(x + offset, SIDE) for offset in ORDER + (0,)]
+    loads = []
+    first = pltpu.make_async_copy(depth_hbm, depth, load_sem.at[2 * chans])
+    first.start()
+    for k, chan in enumerate(channels):
+        pair = [
+            pltpu.make_async_copy(hbm.at[:, chan], vmem.at[:, chan], load_sem.at[2 * k + j])
+            for j, (hbm, vmem) in enumerate(((frames_hbm, frames), (prev_hbm, prev)))
+        ]
+        for copy in pair:
+            copy.start()
+        loads.append(pair)
 
     def of_group(k):
         return (lax.div(k, 2), strip - core + lax.rem(k, 2))
@@ -98,21 +115,72 @@
     partners = [of_group(wrap(group + k, 8)) for k in range(1, 8)]
     partners += [of_y(wrap(y + k, 4)) for k in range(1, 4)]
     partners += [of_z(wrap(z + k, 4)) for k in range(1, 4)]
-    greet(partners)
-    swap_along_x(x, strip, resid, swapped, relay, local_sem, swap_send, swap_recv)
-
-    frames = part.shape[0] * part.shape[1]
+    barrier = pltpu.get_barrier_semaphore()
+    for partner in partners:
+        pl.semaphore_signal(barrier, inc=1, device_id=partner, device_id_type=MESH)
+
+    def residual(chan, write):
+        for f in range(0, count, 8):
+            ok = jnp.where(chan == chans - 1, depth[f : f + 8].astype(F32), 1.0)
+            value = (
+                frames[f : f + 8, chan].astype(F32) - prev[f : f + 8, chan].astype(F32)
+            ) * ok
+            lay(lines, f, value)
+        turned(lines, write, rows)
+
+    args = (x, strip, flat, swapped, swap_send, swap_recv)
+    sends = []
+    first.wait()
+    for k, offset in enumerate(ORDER):
+        for copy in loads[k]:
+            copy.wait()
+
+        def write(where, value, chan=channels[k]):
+            flat[chan, :, where] = value.astype(BF16)
+
+        residual(channels[k], write)
+        if k == 0:
+            pl.semaphore_wait(barrier, len(partners))
+        sends.append(send_along_x(*args, offset))
+        sends[-1].start()
+    for copy in loads[-1]:
+        copy.wait()
+
+    def write_own(where, value):
+        swapped[x, :, where] = value.astype(BF16)
+
+    residual(x, write_own)
+
+    def write_valid(where, value):
+        flat_valid[:, where] = value.astype(BF16)
+
+    lay(lines, 0, depth[...].astype(F32))
+    turned(lines, write_valid, rows)
+    for chan in range(chans):
+
+        def write_frames(where, value):
+            flat_frames[chan, :, where] = value.astype(BF16)
+
+        for f in range(0, count, 8):
+            lay(lines, f, frames[f : f + 8, chan].astype(F32))
+        turned(lines, write_frames, rows)
+    for offset in ORDER:
+        taken_along_x(*args, offset).wait_recv()
+    for copy in sends:
+        copy.wait_send()
+
+    every = part.shape[0] * part.shape[1]
     pixels = swapped.shape[-1]
     chunk = 1024
 
     def add(step, so_far):
         cols = pl.ds(pl.multiple_of(step * chunk, chunk), chunk)
-        block = swapped[:, :, cols].reshape(frames, chunk)
+        block = swapped[:, :, cols].reshape(every, chunk)
         return so_far + lax.dot_general(
             block, block, (((1,), (1,)), ((), ())), preferred_element_type=F32
         )
 
-    partial = lax.fori_loop(0, pixels // chunk, add, jnp.zeros((frames, frames), F32))
+    partial = lax.fori_loop(0, pixels // chunk, add, jnp.zeros((every, every), F32))
     part[...] = partial.reshape(part.shape)
 
     def exchange(index, size, where, source_of, buffer, send_sem, recv_sem):
@@ -171,38 +239,45 @@
     gram[...] = total[...].reshape(gram.shape)
 
 
-def gram_of(resid):
-    chans, count, pixels = resid.shape
-    frames = count * SIDE
-    rows = frames // 8
+def gram_of(frames, prev_fg, depth_valid):
+    count, chans, rows, cols = frames.shape
+    pixels = rows * cols
+    every = count * SIDE
+    piece = every // 8
     dma = pltpu.SemaphoreType.DMA
     return pl.pallas_call(
         gram_kernel,
         out_shape=(
             jax.ShapeDtypeStruct((SIDE, count, pixels), BF16),
-            jax.ShapeDtypeStruct((frames, frames), F32),
+            jax.ShapeDtypeStruct((every, every), F32),
+            jax.ShapeDtypeStruct((chans, count, pixels), BF16),
+            jax.ShapeDtypeStruct((count, pixels), BF16),
         ),
-        in_specs=in_vmem(1),
-        out_specs=tuple(in_vmem(2)),
+        in_specs=[pl.BlockSpec(memory_space=pltpu.HBM)] * 3,
+        out_specs=tuple(in_vmem(4)),
         scratch_shapes=[
-            VMEM((2, count, pixels // 2), BF16),
-            VMEM((8, rows, frames), F32),
-            VMEM((8, rows, frames), F32),
-            VMEM((4, rows, frames), F32),
-            VMEM((4, rows, frames), F32),
-            VMEM((8, rows, frames), F32),
-            dma,
-            dma((6,)), dma((6,)),
+            VMEM(frames.shape, BF16),
+            VMEM(frames.shape, BF16),
+            VMEM(depth_valid.shape, jnp.int32),
+            VMEM((chans, count, pixels), BF16),
+            VMEM((cols // 128, count * rows, 128), F32),
+            VMEM((8, piece, every), F32),
+            VMEM((8, piece, every), F32),
+            VMEM((4, piece, every), F32),
+            VMEM((4, piece, every), F32),
+            VMEM((8, piece, every), F32),
+            dma((2 * chans + 1,)),
+            dma((4,)), dma((4,)),
             dma((8,)), dma((8,)),
             dma((4,)), dma((4,)),
             dma((4,)), dma((4,)),
             dma((8,)), dma((8,)),
         ],
         compiler_params=pltpu.CompilerParams(
-            collective_id=0, has_side_effects=True, vmem_limit_bytes=40 << 20
+            collective_id=0, has_side_effects=True, vmem_limit_bytes=48 << 20
         ),
         name="gram",
-    )(resid)
+    )(frames, prev_fg, depth_valid)
 
 
 def exact(left, right, dims):
@@ -301,92 +376,17 @@
         in_specs=in_vmem(2),
         out_specs=in_vmem(1)[0],
         scratch_shapes=[VMEM((frames, frames), F32), VMEM((rank, frames), F32)],
+        compiler_params=pltpu.CompilerParams(vmem_limit_bytes=4 << 20),
         name="mixing",
     )(gram, sketch.T)
 
 
-def back_kernel(
-    swapped, weights, frames, valid, back, above, below,
-    made, relay, top, bottom, local_sem, swap_send, swap_recv, halo_send, halo_recv,
+def smooth_channel(
+    strips, strip, chan, offset, lam_ref, frames, back, valid, above, below, out,
+    source, first, second, between,
 ):
-    x, strip, _, _, _ = place()
-    strips = lax.axis_size("pix")
-    up, down = wrap(strip - 1, strips), wrap(strip + 1, strips)
-    greet([(wrap(x + 1, SIDE), strip), (wrap(x - 1, SIDE), strip), (x, up), (x, down)])
-    side, count, pixels = swapped.shape
-    chunk = 1024
-    mix = weights[...]
-
-    def multiply(step, carry):
-        cols = pl.ds(pl.multiple_of(step * chunk, chunk), chunk)
-        block = swapped[:, :, cols].reshape(side * count, chunk)
-        out = jnp.dot(mix, block, preferred_element_type=F32)
-        made[:, :, cols] = out.astype(BF16).reshape(side, count, chunk)
-        return carry
-
-    lax.fori_loop(0, pixels // chunk, multiply, 0)
-    swap_along_x(x, strip, made, back, relay, local_sem, swap_send, swap_recv)
-    width = top.shape[-1]
-    for chan in range(side):
-        for target, start in ((top, 0), (bottom, pixels - width)):
-            cols = slice(start, start + width)
-            source = frames[chan, :, cols].astype(F32) - back[chan, :, cols].astype(F32)
-            if chan == side - 1:
-                source = source * valid[:, cols].astype(F32)
-            target[chan] = source.astype(BF16)
-    copies = []
-    for k, (source, target, to) in enumerate(((top, below, up), (bottom, above, down))):
-        copies.append(
-            pltpu.make_async_remote_copy(
-                src_ref=source,
-                dst_ref=target,
-                send_sem=halo_send.at[k],
-                recv_sem=halo_recv.at[k],
-                device_id=(x, to),
-                device_id_type=MESH,
-            )
-        )
-    for copy in copies:
-        copy.start()
-    for copy in copies:
-        copy.wait()
-
-
-def back_of(swapped, weights, frames, valid, cols):
-    side, count, pixels = swapped.shape
-    dma = pltpu.SemaphoreType.DMA
-    halo = (side, count, NSWEEP * cols)
-    return pl.pallas_call(
-        back_kernel,
-        out_shape=(
-            jax.ShapeDtypeStruct(swapped.shape, BF16),
-            jax.ShapeDtypeStruct(halo, BF16),
-            jax.ShapeDtypeStruct(halo, BF16),
-        ),
-        in_specs=in_vmem(4),
-        out_specs=tuple(in_vmem(3)),
-        scratch_shapes=[
-            VMEM(swapped.shape, BF16),
-            VMEM((2, count, pixels // 2), BF16),
-            VMEM(halo, BF16),
-            VMEM(halo, BF16),
-            dma,
-            dma((6,)), dma((6,)),
-            dma((2,)), dma((2,)),
-        ],
-        compiler_params=pltpu.CompilerParams(
-            collective_id=1, has_side_effects=True, vmem_limit_bytes=40 << 20
-        ),
-        name="back",
-    )(swapped, weights, frames, valid)
-
-
-def tv_kernel(strips, strip_ref, lam_ref, frames, back, valid, above, below, out, source, first, second):
-    chan = pl.program_id(0)
-    last = pl.num_programs(0) - 1
-    lam = lam_ref[chan]
-    inverse = 1.0 / lam
-    strip = strip_ref[0]
+    inverse = 1.0 / lam_ref[chan]
+    last = frames.shape[0] - 1
     halo = NSWEEP
     span, lines, cols = source.shape
     rows = span - 2 * halo
@@ -403,12 +403,12 @@
             ref[r, :, 128 * j : 128 * j + 128] = values[j]
 
     for r in range(halo):
-        source[r] = above[0, :, r * cols : (r + 1) * cols].astype(F32) * 0.125
-        source[halo + rows + r] = below[0, :, r * cols : (r + 1) * cols].astype(F32) * 0.125
+        source[r] = above[offset, :, r * cols : (r + 1) * cols].astype(F32) * 0.125
+        source[halo + rows + r] = below[offset, :, r * cols : (r + 1) * cols].astype(F32) * 0.125
     for r in range(rows):
         where = slice(r * cols, (r + 1) * cols)
         ok = jnp.where(chan == last, valid[:, where].astype(F32), 1.0)
-        source[halo + r] = (frames[0, :, where].astype(F32) - back[0, :, where].astype(F32)) * (ok * 0.125)
+        source[halo + r] = (frames[chan, :, where].astype(F32) - back[chan, :, where].astype(F32)) * (ok * 0.125)
 
     def before(values):
         turned = [pltpu.roll(v, 1, 1) for v in values]
@@ -446,6 +446,8 @@
         update(r, smooth, under, None, None)
         smooth = under
     for sweep in range(1, NSWEEP):
+        if sweep == 3:
+            between()
         here, beside = tile(first, sweep), tile(second, sweep)
         smooth = image(sweep, tile(first, sweep - 1), here, beside)
         for r in range(sweep, span - 1 - sweep):
@@ -457,56 +459,175 @@
         i = halo + r
         values = image(i, tile(first, i - 1), tile(first, i), tile(second, i))
         for j in range(tiles):
-            out[0, :, r * cols + 128 * j : r * cols + 128 * j + 128] = (values[j] * 8.0).astype(BF16)
-
-
-def foreground_of(frames, back, valid, above, below, lam, strip, strips, cols):
-    chans, count, pixels = frames.shape
-    lines = 32
-    rows = pixels // cols
-    span = rows + 2 * NSWEEP
-    whole = pl.BlockSpec((1, lines, pixels), lambda c, f, *_: (c, f, 0))
-    edge = pl.BlockSpec((1, lines, NSWEEP * cols), lambda c, f, *_: (c, f, 0))
-    scalar = pl.BlockSpec(memory_space=pltpu.SMEM)
+            out[chan, :, r * cols + 128 * j : r * cols + 128 * j + 128] = (values[j] * 8.0).astype(BF16)
+
+
+def finish_kernel(
+    lam_ref, swapped, weights, frames, valid, back, fore,
+    made, top, bottom, above, below, source, first, second,
+    local_sem, swap_send, swap_recv, halo_send, halo_recv,
+):
+    x, strip, _, _, _ = place()
+    strips = lax.axis_size("pix")
+    up, down = wrap(strip - 1, strips), wrap(strip + 1, strips)
+    partners = [(wrap(x + k, SIDE), strip) for k in ORDER] + [(x, up), (x, down)]
+    barrier = pltpu.get_barrier_semaphore()
+    for partner in partners:
+        pl.semaphore_signal(barrier, inc=1, device_id=partner, device_id_type=MESH)
+    side, count, pixels = swapped.shape
+    width = top.shape[-1]
+    cols = source.shape[-1]
+    parts = ((0, width), (pixels - width, width), (width, pixels - 2 * width))
+    mix = weights[...]
+
+    def multiply(part):
+        start, size = parts[part]
+        for at in range(start, start + size, 512):
+            where = slice(at, at + 512)
+            block = swapped[:, :, where].reshape(side * count, 512)
+            out = jnp.dot(mix, block, preferred_element_type=F32)
+            made[:, :, where] = out.astype(BF16).reshape(side, count, 512)
+
+    def send(offset, part):
+        to = wrap(x + offset, SIDE)
+        where = pl.ds(*parts[part])
+        return pltpu.make_async_remote_copy(
+            src_ref=made.at[to, :, where],
+            dst_ref=back.at[x, :, where],
+            send_sem=swap_send.at[offset, part],
+            recv_sem=swap_recv.at[offset, part],
+            device_id=(to, strip),
+            device_id_type=MESH,
+        )
+
+    def taken(offset, part):
+        origin = wrap(x - offset, SIDE)
+        where = pl.ds(*parts[part])
+        return pltpu.make_async_remote_copy(
+            src_ref=made.at[origin, :, where],
+            dst_ref=back.at[origin, :, where],
+            send_sem=swap_send.at[offset, part],
+            recv_sem=swap_recv.at[offset, part],
+            device_id=(origin, strip),
+            device_id_type=MESH,
+        )
+
+    def halo(offset, way):
+        outgoing, incoming, to = ((top, below, up), (bottom, above, down))[way]
+        return pltpu.make_async_remote_copy(
+            src_ref=outgoing.at[offset],
+            dst_ref=incoming.at[offset],
+            send_sem=halo_send.at[offset, way],
+            recv_sem=halo_recv.at[offset, way],
+            device_id=(x, to),
+            device_id_type=MESH,
+        )
+
+    def forward(offset):
+        chan = wrap(x - offset, SIDE)
+        if offset:
+            taken(offset, 0).wait_recv()
+            taken(offset, 1).wait_recv()
+        for way, target in ((0, top), (1, bottom)):
+            where = slice(parts[way][0], parts[way][0] + width)
+            held = back if offset else made
+            edge = frames[chan, :, where].astype(F32) - held[chan, :, where].astype(F32)
+            ok = jnp.where(chan == side - 1, valid[:, where].astype(F32), 1.0)
+            target[offset] = (edge * ok).astype(BF16)
+        for way in range(2):
+            halo(offset, way).start()
+
+    multiply(0)
+    multiply(1)
+    pl.semaphore_wait(barrier, len(partners))
+    forward(0)
+    for offset in (1, 3):
+        for part in range(2):
+            send(offset, part).start()
+    multiply(2)
+    for offset in (1, 3):
+        send(offset, 2).start()
+    for part in (0, 1, 2):
+        send(2, part).start()
+    mine = pltpu.make_async_copy(made.at[x], back.at[x], local_sem)
+    mine.start()
+    mine.wait()
+
+    def group(k, carry):
+        offset = k + jnp.where(k == 2, 1, 0) - jnp.where(k == 3, 1, 0)
+
+        @pl.when(k > 0)
+        def _():
+            taken(offset, 2).wait_recv()
+
+        for way in range(2):
+            halo(offset, way).wait_recv()
+
+        def between():
+            @pl.when(k == 0)
+            def _():
+                forward(1)
+                forward(3)
+
+            @pl.when(k == 1)
+            def _():
+                forward(2)
+
+        smooth_channel(
+            strips, strip, wrap(x - offset, SIDE), offset, lam_ref,
+            frames, back, valid, above, below, fore, source, first, second, between,
+        )
+        return carry
+
+    lax.fori_loop(0, SIDE, group, 0)
+    for offset in ORDER:
+        for part in range(3):
+            send(offset, part).wait_send()
+    for offset in range(SIDE):
+        for way in range(2):
+            halo(offset, way).wait_send()
+
+
+def finish_of(swapped, weights, frames, valid, lam, cols):
+    side, count, pixels = swapped.shape
+    dma = pltpu.SemaphoreType.DMA
+    edge = (side, count, NSWEEP * cols)
+    field = (pixels // cols + 2 * NSWEEP, count, cols)
     return pl.pallas_call(
-        functools.partial(tv_kernel, strips),
-        grid=(chans, count // lines),
-        out_shape=jax.ShapeDtypeStruct(frames.shape, BF16),
-        in_specs=[
-            scalar,
-            scalar,
-            whole,
-            whole,
-            pl.BlockSpec((lines, pixels), lambda c, f: (f, 0)),
-            edge,
-            edge,
+        finish_kernel,
+        out_shape=(
+            jax.ShapeDtypeStruct(swapped.shape, BF16),
+            jax.ShapeDtypeStruct(swapped.shape, BF16),
+        ),
+        in_specs=[pl.BlockSpec(memory_space=pltpu.SMEM)] + in_vmem(4),
+        out_specs=tuple(in_vmem(2)),
+        scratch_shapes=[
+            VMEM(swapped.shape, BF16),
+            VMEM(edge, BF16),
+            VMEM(edge, BF16),
+            VMEM(edge, BF16),
+            VMEM(edge, BF16),
+            VMEM(field, F32),
+            VMEM(field, F32),
+            VMEM(field, F32),
+            dma,
+            dma((4, 3)), dma((4, 3)),
+            dma((4, 2)), dma((4, 2)),
         ],
-        out_specs=whole,
-        scratch_shapes=[VMEM((span, lines, cols), F32)] * 3,
-        compiler_params=pltpu.CompilerParams(vmem_limit_bytes=40 << 20),
-        name="tv",
-    )(strip, lam, frames, back, valid, above, below)
+        compiler_params=pltpu.CompilerParams(
+            collective_id=1, has_side_effects=True, vmem_limit_bytes=32 << 20
+        ),
+        name="finish",
+    )(lam, swapped, weights, frames, valid)
 
 
 def local(frames, prev_fg, depth_valid, sketch, tv_weight):
     count, chans, rows, cols = frames.shape
     strips = lax.axis_size("pix")
     nval = chans * rows * strips * cols
-    chan_ids = lax.broadcasted_iota(jnp.int32, (1, chans, 1, 1), 1)
-    depth_ok = depth_valid[:, None, :, :].astype(F32)
-    valid = jnp.where(chan_ids == chans - 1, depth_ok, F32(1.0))
-    resid = ((frames.astype(F32) - prev_fg.astype(F32)) * valid).astype(BF16)
-
-    def flat(value):
-        return value.transpose(1, 0, 2, 3).reshape(chans, count, rows * cols)
-
-    resid, frames = flat(resid), flat(frames)
-    ok = depth_valid.astype(BF16).reshape(count, rows * cols)
-    swapped, gram = gram_of(resid)
+    swapped, gram, frames, ok = gram_of(frames, prev_fg, depth_valid)
     weights = mixing_of(gram, sketch, nval)
-    back, above, below = back_of(swapped, weights, frames, ok, cols)
-    strip = lax.axis_index("pix").reshape(1)
-    fore = foreground_of(frames, back, ok, above, below, tv_weight, strip, strips, cols)
+    back, fore = finish_of(swapped, weights, frames, ok, tv_weight, cols)
 
     def unflat(value):
         return value.reshape(chans, count, rows, cols).transpose(1, 0, 2, 3)

time: 149 us -> 104 us (0.70)
  Pallas kernels: 123 us -> 96.8 us
  local copies, waits for them, and re-layouts: 16.8 us -> 5.54 us
  other arithmetic: 6.09 us -> 0 us
    pallas_call x2 -> x1, Pallas kernels: 64.9 us -> 40 us  [finish_of(): pl.pallas_call(finish_kernel, out_shape=(jax.ShapeDtypeStruct(swapped.sha...]
    reshape x4 -> x0, local copies, waits for them, and re-layouts: 11.7 us -> none  [flat(): return value.transpose(1, 0, 2, 3).reshape(chans, count, rows * cols)]
    transpose x1 -> x0, other arithmetic: 4.14 us -> none  [flat(): return value.transpose(1, 0, 2, 3).reshape(chans, count, rows * cols)]
    convert_element_type x1 -> x0, other arithmetic: 1.95 us -> none  [local(): ok = depth_valid.astype(BF16).reshape(count, rows * cols)]
where the time goes in v3:
time: 104 us; the launch traced here: 103 us
  Pallas kernels  96.8 us (93%)
  local copies, waits for them, and re-layouts  5.54 us (5%)
    pallas_call x1, Pallas kernels, gram_of(): pl.pallas_call(gram_kernel, out_shape=(jax.ShapeDtypeStruct((SIDE, count,...  47.1 us
    pallas_call x1, Pallas kernels, finish_of(): pl.pallas_call(finish_kernel, out_shape=(jax.ShapeDtypeStruct(swapped.sha...  40 us
    pallas_call x1, Pallas kernels, mixing_of(): pl.pallas_call(functools.partial(mixing_kernel, nval), out_shape=jax.Shap...  9.61 us
    unnamed x8, local copies, waits for them, and re-layouts  2.89 us
    transpose x1, local copies, waits for them, and re-layouts, unflat(): return value.reshape(chans, count, rows, cols).transpose(1, 0, 2, 3)  2.65 us

profile of v3, /device:TPU:6, one launch (start us, length us, event | category | flops | bytes accessed | tf_op | source)
XLA Modules:
  0.0 103.0 jit_solution(14042079583967856648)
XLA Ops:
  0.6 0.0 copy-start
  0.6 1.2 %copy-done = s32[32,16,512]{2,1,0:T(8,128)S(1)} copy-done((s32[32,16,512]{2,1,0:T(8,128)S(1)}, s32[32,16,512]{2,1,0:T(8,128)}, u32[]{:S(2)}) %copy-start) | copy-done | bytes 1048600
  1.9 0.0 copy-start.1
  1.9 0.0 copy-start.2
  1.9 47.1 %gram.1 = (bf16[4,32,8192]{2,1,0:T(8,128)(2,1)S(1)}, f32[128,128]{1,0:T(8,128)S(1)}, bf16[4,32,8192]{2,1,0:T(8,128)(2,1)S(1)}, bf16[32,8192]{1,0:T(8,128)(2,1)S(1)}) custom-call(bf16[32,4,16,512]{3,2,1,0:T(8,128)(2,1)} %frames_hbm.1, bf16[32,4,16,512]{3,2,1,0:T(8,128)(2,1)} %prev_hbm.1, s32[32,16,512]{2,1,0:T(8,128)S(1)} %copy-done), custom_call_target="tpu_custom_call" | custom-call | tf_op jit(solution)/shard_map/gram/pallas_call | solution.py:248
  49.0 0.0 copy-done.1
  49.0 9.6 %mixing.1.weights = bf16[128,128]{1,0:T(8,128)(2,1)S(1)} custom-call(f32[128,128]{1,0:T(8,128)S(1)} %get-tuple-element.9.gram_ref, f32[64,128]{1,0:T(8,128)S(1)} %bitcast.23), custom_call_target="tpu_custom_call" | custom-call | tf_op jit(solution)/shard_map/mixing/pallas_call | solution.py:373
  58.6 0.0 copy-done.2
  58.7 40.0 %finish.1 = (bf16[4,32,8192]{2,1,0:T(8,128)(2,1)S(1)}, bf16[4,32,8192]{2,1,0:T(8,128)(2,1)S(1)}) custom-call(f32[4]{0:T(128)S(1)} %copy-done.2, bf16[4,32,8192]{2,1,0:T(8,128)(2,1)S(1)} %get-tuple-element.8.swapped, bf16[128,128]{1,0:T(8,128)(2,1)S(1)} %mixing.1.weights, bf16[4,32,8192]{2,1,0:T(8,128)(2,1)S(1)} %get-tuple-element.10.frames, ...), custom_call_target="tpu_custom_call" | custom-call | tf_op jit(solution)/shard_map/finish/pallas_call | solution.py:596
  98.7 0.8 copy.9
  99.5 0.8 copy.10
  100.4 2.7 %copy_bitcast_fusion = (bf16[32,4,16,512]{3,2,1,0:T(8,128)(2,1)}, bf16[32,4,16,512]{3,2,1,0:T(8,128)(2,1)}) fusion(bf16[4,32,16,512]{3,2,1,0:T(8,128)(2,1)S(1)} %bitcast.24, bf16[4,32,16,512]{3,2,1,0:T(8,128)(2,1)S(1)} %bitcast.25), kind=kLoop, calls=%fused_computation | loop fusion | bytes 8388608 | tf_op jit(solution)/shard_map/transpose | solution.py:633
Async XLA Ops:
  0.6 1.2 %copy-start = (s32[32,16,512]{2,1,0:T(8,128)S(1)}, s32[32,16,512]{2,1,0:T(8,128)}, u32[]{:S(2)}) copy-start(s32[32,16,512]{2,1,0:T(8,128)} %depth_hbm.1) | copy-start | bytes 3145732
  1.9 47.2 %copy-start.1 = (f32[128,64]{0,1:T(8,128)S(1)}, f32[128,64]{0,1:T(8,128)}, u32[]{:S(2)}) copy-start(f32[128,64]{0,1:T(8,128)} %param.8) | copy-start | bytes 98308
  1.9 56.8 %copy-start.2 = (f32[4]{0:T(128)S(1)}, f32[4]{0:T(128)}, u32[]{:S(2)}) copy-start(f32[4]{0:T(128)} %lam_ref.1) | copy-start | bytes 52

commit v4 on v3

--- a/solution.py
+++ b/solution.py
@@ -31,32 +31,25 @@
     return x, strip, lax.div(strip, 8), lax.rem(lax.div(strip, 2), 4), lax.rem(strip, 2)
 
 
-def greet(partners):
-    barrier = pltpu.get_barrier_semaphore()
-    for partner in partners:
-        pl.semaphore_signal(barrier, inc=1, device_id=partner, device_id_type=MESH)
-    pl.semaphore_wait(barrier, len(partners))
-
-
-def send_along_x(x, strip, src, dst, send_sem, recv_sem, offset):
+def send_along_x(x, strip, src, dst, send_sem, recv_sem, offset, part, where):
     to = wrap(x + offset, SIDE)
     return pltpu.make_async_remote_copy(
-        src_ref=src.at[to],
-        dst_ref=dst.at[x],
-        send_sem=send_sem.at[offset],
-        recv_sem=recv_sem.at[offset],
+        src_ref=src.at[to, :, where],
+        dst_ref=dst.at[x, :, where],
+        send_sem=send_sem.at[offset, part],
+        recv_sem=recv_sem.at[offset, part],
         device_id=(to, strip),
         device_id_type=MESH,
     )
 
 
-def taken_along_x(x, strip, src, dst, send_sem, recv_sem, offset):
+def taken_along_x(x, strip, src, dst, send_sem, recv_sem, offset, part, where):
     origin = wrap(x - offset, SIDE)
     return pltpu.make_async_remote_copy(
-        src_ref=src.at[origin],
-        dst_ref=dst.at[origin],
-        send_sem=send_sem.at[offset],
-        recv_sem=recv_sem.at[offset],
+        src_ref=src.at[origin, :, where],
+        dst_ref=dst.at[origin, :, where],
+        send_sem=send_sem.at[offset, part],
+        recv_sem=recv_sem.at[offset, part],
         device_id=(origin, strip),
         device_id_type=MESH,
     )
@@ -81,9 +74,8 @@
             write(slice(start, start + 128), value)
 
 
-def gram_kernel(
-    frames_hbm, prev_hbm, depth_hbm, swapped, gram, flat_frames, flat_valid,
-    frames, prev, depth, flat, lines, part, pieces, in_y, in_z, total,
+def gram_stage(
+    frames_hbm, prev_hbm, depth_hbm, swapped, flat_frames, flat_valid, frames, prev, depth, flat, lines, part, pieces, in_y, in_z, total,
     load_sem, swap_send, swap_recv, first_send, first_recv, y_send, y_recv, z_send, z_recv,
     last_send, last_recv,
 ):
@@ -115,6 +107,8 @@
     partners = [of_group(wrap(group + k, 8)) for k in range(1, 8)]
     partners += [of_y(wrap(y + k, 4)) for k in range(1, 4)]
     partners += [of_z(wrap(z + k, 4)) for k in range(1, 4)]
+    strips = lax.axis_size("pix")
+    partners += [(x, wrap(strip + k, strips)) for k in (-1, 1)]
     barrier = pltpu.get_barrier_semaphore()
     for partner in partners:
         pl.semaphore_signal(barrier, inc=1, device_id=partner, device_id_type=MESH)
@@ -129,6 +123,8 @@
         turned(lines, write, rows)
 
     args = (x, strip, flat, swapped, swap_send, swap_recv)
+    pixels = rows * cols
+    halves = (pl.ds(0, pixels // 2), pl.ds(pixels // 2, pixels // 2))
     sends = []
     first.wait()
     for k, offset in enumerate(ORDER):
@@ -141,7 +137,10 @@
         residual(channels[k], write)
         if k == 0:
             pl.semaphore_wait(barrier, len(partners))
-        sends.append(send_along_x(*args, offset))
+        sends.append(send_along_x(*args, offset, 0, halves[0]))
+        sends[-1].start()
+    for offset in ORDER:
+        sends.append(send_along_x(*args, offset, 1, halves[1]))
         sends[-1].start()
     for copy in loads[-1]:
         copy.wait()
@@ -164,23 +163,19 @@
         for f in range(0, count, 8):
             lay(lines, f, frames[f : f + 8, chan].astype(F32))
         turned(lines, write_frames, rows)
-    for offset in ORDER:
-        taken_along_x(*args, offset).wait_recv()
+    every = count * SIDE
+    chunk = 1024
+    partial = jnp.zeros((every, every), F32)
+    for half in range(2):
+        for offset in ORDER:
+            taken_along_x(*args, offset, half, halves[half]).wait_recv()
+        for start in range(half * pixels // 2, (half + 1) * pixels // 2, chunk):
+            block = swapped[:, :, start : start + chunk].reshape(every, chunk)
+            partial = partial + lax.dot_general(
+                block, block, (((1,), (1,)), ((), ())), preferred_element_type=F32
+            )
     for copy in sends:
         copy.wait_send()
-
-    every = part.shape[0] * part.shape[1]
-    pixels = swapped.shape[-1]
-    chunk = 1024
-
-    def add(step, so_far):
-        cols = pl.ds(pl.multiple_of(step * chunk, chunk), chunk)
-        block = swapped[:, :, cols].reshape(every, chunk)
-        return so_far + lax.dot_general(
-            block, block, (((1,), (1,)), ((), ())), preferred_element_type=F32
-        )
-
-    partial = lax.fori_loop(0, pixels // chunk, add, jnp.zeros((every, every), F32))
     part[...] = partial.reshape(part.shape)
 
     def exchange(index, size, where, source_of, buffer, send_sem, recv_sem):
@@ -236,48 +231,7 @@
 
     args = (group, 8, of_group, lambda k: total.at[group], total, last_send, last_recv)
     arrive(*args, exchange(*args))
-    gram[...] = total[...].reshape(gram.shape)
-
-
-def gram_of(frames, prev_fg, depth_valid):
-    count, chans, rows, cols = frames.shape
-    pixels = rows * cols
-    every = count * SIDE
-    piece = every // 8
-    dma = pltpu.SemaphoreType.DMA
-    return pl.pallas_call(
-        gram_kernel,
-        out_shape=(
-            jax.ShapeDtypeStruct((SIDE, count, pixels), BF16),
-            jax.ShapeDtypeStruct((every, every), F32),
-            jax.ShapeDtypeStruct((chans, count, pixels), BF16),
-            jax.ShapeDtypeStruct((count, pixels), BF16),
-        ),
-        in_specs=[pl.BlockSpec(memory_space=pltpu.HBM)] * 3,
-        out_specs=tuple(in_vmem(4)),
-        scratch_shapes=[
-            VMEM(frames.shape, BF16),
-            VMEM(frames.shape, BF16),
-            VMEM(depth_valid.shape, jnp.int32),
-            VMEM((chans, count, pixels), BF16),
-            VMEM((cols // 128, count * rows, 128), F32),
-            VMEM((8, piece, every), F32),
-            VMEM((8, piece, every), F32),
-            VMEM((4, piece, every), F32),
-            VMEM((4, piece, every), F32),
-            VMEM((8, piece, every), F32),
-            dma((2 * chans + 1,)),
-            dma((4,)), dma((4,)),
-            dma((8,)), dma((8,)),
-            dma((4,)), dma((4,)),
-            dma((4,)), dma((4,)),
-            dma((8,)), dma((8,)),
-        ],
-        compiler_params=pltpu.CompilerParams(
-            collective_id=0, has_side_effects=True, vmem_limit_bytes=48 << 20
-        ),
-        name="gram",
-    )(frames, prev_fg, depth_valid)
+    return total[...].reshape(every, every)
 
 
 def exact(left, right, dims):
@@ -349,9 +303,9 @@
     return [jnp.concatenate(out, axis=0) for out in solved]
 
 
-def mixing_kernel(nval, gram_ref, sketch_ref, mixing_ref, gram_sc, basis_sc):
-    gram_sc[...] = gram_ref[...] * (1.0 / nval)
-    basis_sc[...] = sketch_ref[...]
+def mixing_stage(gram, sketch, gram_sc, basis_sc):
+    gram_sc[...] = gram
+    basis_sc[...] = sketch
 
     def turn(step, carry):
         basis = basis_sc[...]
@@ -365,27 +319,15 @@
     image = exact(basis, gram_sc[...], ((1,), (0,)))
     square = exact(basis, image, ((1,), (1,)))
     left, right = lower_solve(square, [basis, image])
-    mixing_ref[...] = exact(right, left, ((0,), (0,))).astype(BF16)
-
-
-def mixing_of(gram, sketch, nval):
-    frames, rank = sketch.shape
-    return pl.pallas_call(
-        functools.partial(mixing_kernel, nval),
-        out_shape=jax.ShapeDtypeStruct((frames, frames), BF16),
-        in_specs=in_vmem(2),
-        out_specs=in_vmem(1)[0],
-        scratch_shapes=[VMEM((frames, frames), F32), VMEM((rank, frames), F32)],
-        compiler_params=pltpu.CompilerParams(vmem_limit_bytes=4 << 20),
-        name="mixing",
-    )(gram, sketch.T)
+    return exact(right, left, ((0,), (0,))).astype(BF16)
 
 
 def smooth_channel(
-    strips, strip, chan, offset, lam_ref, frames, back, valid, above, below, out,
-    source, first, second, between,
+    strips, strip, chan, offset, lam_ref, frames, back, valid, above, below,
+    back_out, fore_out, lines_out, source, first, second, between,
 ):
-    inverse = 1.0 / lam_ref[chan]
+    lam = lam_ref[chan]
+    step = STEP_SIZE / lam
     last = frames.shape[0] - 1
     halo = NSWEEP
     span, lines, cols = source.shape
@@ -402,13 +344,25 @@
         for j in range(tiles):
             ref[r, :, 128 * j : 128 * j + 128] = values[j]
 
+    def unturn(r, values):
+        for j in range(tiles):
+            lines_out.at[j][pl.ds(r, lines, stride=rows), :] = values[j]
+
+    def unlay(target):
+        for j in range(tiles):
+            value = lines_out[j].reshape(lines, rows, 128).astype(BF16)
+            target[:, chan, :, 128 * j : 128 * j + 128] = value
+
     for r in range(halo):
-        source[r] = above[offset, :, r * cols : (r + 1) * cols].astype(F32) * 0.125
-        source[halo + rows + r] = below[offset, :, r * cols : (r + 1) * cols].astype(F32) * 0.125
+        source[r] = above[offset, :, r * cols : (r + 1) * cols].astype(F32) * step
+        source[halo + rows + r] = below[offset, :, r * cols : (r + 1) * cols].astype(F32) * step
     for r in range(rows):
         where = slice(r * cols, (r + 1) * cols)
         ok = jnp.where(chan == last, valid[:, where].astype(F32), 1.0)
-        source[halo + r] = (frames[chan, :, where].astype(F32) - back[chan, :, where].astype(F32)) * (ok * 0.125)
+        held = back[chan, :, where].astype(F32)
+        unturn(r, [held[:, 128 * j : 128 * j + 128] for j in range(tiles)])
+        source[halo + r] = (frames[chan, :, where].astype(F32) - held) * (ok * step)
+    unlay(back_out)
 
     def before(values):
         turned = [pltpu.roll(v, 1, 1) for v in values]
@@ -418,9 +372,9 @@
         turned = [pltpu.roll(v, 127, 1) for v in values]
         return [jnp.where(lane == 127, turned[j + 1] if j + 1 < tiles else values[j], turned[j]) for j in range(tiles)]
 
-    def image(r, up, here, beside, scale=0.125):
+    def image(r, up, here, beside):
         left = before(beside)
-        return [s - scale * ((h - u) + (b - l)) for s, u, h, b, l in zip(tile(source, r), up, here, beside, left)]
+        return [s - STEP_SIZE * ((h - u) + (b - l)) for s, u, h, b, l in zip(tile(source, r), up, here, beside, left)]
 
     def update(r, smooth, under, here, beside):
         right = after(smooth)
@@ -433,7 +387,7 @@
                 down = down * open_below
             across = right[j] - smooth[j]
             square = jnp.maximum(down * down + across * across, 1e-37)
-            rate = 1.0 / (1.0 + inverse * (square * lax.rsqrt(square)))
+            rate = 1.0 / (1.0 + square * lax.rsqrt(square))
             a = -down if here is None else here[j] - down
             b = -across if beside is None else beside[j] - across
             news.append((a * rate, b * rate))
@@ -446,8 +400,7 @@
         update(r, smooth, under, None, None)
         smooth = under
     for sweep in range(1, NSWEEP):
-        if sweep == 3:
-            between()
+        between(sweep)
         here, beside = tile(first, sweep), tile(second, sweep)
         smooth = image(sweep, tile(first, sweep - 1), here, beside)
         for r in range(sweep, span - 1 - sweep):
@@ -458,27 +411,22 @@
     for r in range(rows):
         i = halo + r
         values = image(i, tile(first, i - 1), tile(first, i), tile(second, i))
-        for j in range(tiles):
-            out[chan, :, r * cols + 128 * j : r * cols + 128 * j + 128] = (values[j] * 8.0).astype(BF16)
-
-
-def finish_kernel(
-    lam_ref, swapped, weights, frames, valid, back, fore,
-    made, top, bottom, above, below, source, first, second,
+        unturn(r, [v * (lam * (1.0 / STEP_SIZE)) for v in values])
+    unlay(fore_out)
+
+
+def finish_stage(
+    lam_ref, swapped, mix, frames, valid, back_out, fore_out, lines_out,
+    back, made, top, bottom, above, below, source, first, second,
     local_sem, swap_send, swap_recv, halo_send, halo_recv,
 ):
     x, strip, _, _, _ = place()
     strips = lax.axis_size("pix")
     up, down = wrap(strip - 1, strips), wrap(strip + 1, strips)
-    partners = [(wrap(x + k, SIDE), strip) for k in ORDER] + [(x, up), (x, down)]
-    barrier = pltpu.get_barrier_semaphore()
-    for partner in partners:
-        pl.semaphore_signal(barrier, inc=1, device_id=partner, device_id_type=MESH)
     side, count, pixels = swapped.shape
     width = top.shape[-1]
     cols = source.shape[-1]
     parts = ((0, width), (pixels - width, width), (width, pixels - 2 * width))
-    mix = weights[...]
 
     def multiply(part):
         start, size = parts[part]
@@ -539,7 +487,6 @@
 
     multiply(0)
     multiply(1)
-    pl.semaphore_wait(barrier, len(partners))
     forward(0)
     for offset in (1, 3):
         for part in range(2):
@@ -563,19 +510,19 @@
         for way in range(2):
             halo(offset, way).wait_recv()
 
-        def between():
-            @pl.when(k == 0)
-            def _():
-                forward(1)
-                forward(3)
-
-            @pl.when(k == 1)
-            def _():
-                forward(2)
+        def between(sweep):
+            for turn, at, offsets in ((0, 3, (1, 3)), (2, 1, (2,))):
+                if sweep == at:
+
+                    @pl.when(k == turn)
+                    def _():
+                        for offset in offsets:
+                            forward(offset)
 
         smooth_channel(
             strips, strip, wrap(x - offset, SIDE), offset, lam_ref,
-            frames, back, valid, above, below, fore, source, first, second, between,
+            frames, back, valid, above, below, back_out, fore_out, lines_out,
+            source, first, second, between,
         )
         return carry
 
@@ -588,51 +535,81 @@
             halo(offset, way).wait_send()
 
 
-def finish_of(swapped, weights, frames, valid, lam, cols):
-    side, count, pixels = swapped.shape
+def whole_kernel(nval, lam_ref, frames_hbm, prev_hbm, depth_hbm, sketch, back, fore, *scratch):
+    swapped, flat_frames, flat_valid = scratch[:3]
+    gram = gram_stage(frames_hbm, prev_hbm, depth_hbm, *scratch[:24])
+    mix = mixing_stage(gram * (1.0 / nval), sketch[...], *scratch[24:26])
+    finish_stage(
+        lam_ref, swapped, mix, flat_frames, flat_valid, back, fore, scratch[7], *scratch[26:]
+    )
+
+
+def low_rank_and_rest(frames, prev_fg, depth_valid, sketch, lam, nval):
+    count, chans, rows, cols = frames.shape
+    pixels = rows * cols
+    every = count * SIDE
+    piece = every // 8
+    rank = sketch.shape[1]
     dma = pltpu.SemaphoreType.DMA
-    edge = (side, count, NSWEEP * cols)
-    field = (pixels // cols + 2 * NSWEEP, count, cols)
+    flat = (chans, count, pixels)
+    edge = (chans, count, NSWEEP * cols)
+    field = (rows + 2 * NSWEEP, count, cols)
+    gram_scratch = [
+        VMEM(flat, BF16),
+        VMEM(flat, BF16),
+        VMEM((count, pixels), BF16),
+        VMEM(frames.shape, BF16),
+        VMEM(frames.shape, BF16),
+        VMEM(depth_valid.shape, jnp.int32),
+        VMEM(flat, BF16),
+        VMEM((cols // 128, count * rows, 128), F32),
+        VMEM((8, piece, every), F32),
+        VMEM((8, piece, every), F32),
+        VMEM((4, piece, every), F32),
+        VMEM((4, piece, every), F32),
+        VMEM((8, piece, every), F32),
+        dma((2 * chans + 1,)),
+        dma((4, 2)), dma((4, 2)),
+        dma((8,)), dma((8,)),
+        dma((4,)), dma((4,)),
+        dma((4,)), dma((4,)),
+        dma((8,)), dma((8,)),
+    ]
+    mixing_scratch = [VMEM((every, every), F32), VMEM((rank, every), F32)]
+    finish_scratch = [
+        VMEM(flat, BF16),
+        VMEM(flat, BF16),
+        VMEM(edge, BF16),
+        VMEM(edge, BF16),
+        VMEM(edge, BF16),
+        VMEM(edge, BF16),
+        VMEM(field, F32),
+        VMEM(field, F32),
+        VMEM(field, F32),
+        dma,
+        dma((4, 3)), dma((4, 3)),
+        dma((4, 2)), dma((4, 2)),
+    ]
     return pl.pallas_call(
-        finish_kernel,
-        out_shape=(
-            jax.ShapeDtypeStruct(swapped.shape, BF16),
-            jax.ShapeDtypeStruct(swapped.shape, BF16),
+        functools.partial(whole_kernel, nval),
+        out_shape=(jax.ShapeDtypeStruct(frames.shape, BF16),) * 2,
+        in_specs=[pl.BlockSpec(memory_space=pltpu.SMEM)]
+        + [pl.BlockSpec(memory_space=pltpu.HBM)] * 3
+        + in_vmem(1),
+        out_specs=tuple(in_vmem(2)),
+        scratch_shapes=gram_scratch + mixing_scratch + finish_scratch,
+        compiler_params=pltpu.CompilerParams(
+            collective_id=0, has_side_effects=True, vmem_limit_bytes=48 << 20
         ),
-        in_specs=[pl.BlockSpec(memory_space=pltpu.SMEM)] + in_vmem(4),
-        out_specs=tuple(in_vmem(2)),
-        scratch_shapes=[
-            VMEM(swapped.shape, BF16),
-            VMEM(edge, BF16),
-            VMEM(edge, BF16),
-            VMEM(edge, BF16),
-            VMEM(edge, BF16),
-            VMEM(field, F32),
-            VMEM(field, F32),
-            VMEM(field, F32),
-            dma,
-            dma((4, 3)), dma((4, 3)),
-            dma((4, 2)), dma((4, 2)),
-        ],
-        compiler_params=pltpu.CompilerParams(
-            collective_id=1, has_side_effects=True, vmem_limit_bytes=32 << 20
-        ),
-        name="finish",
-    )(lam, swapped, weights, frames, valid)
+        name="godec",
+    )(lam, frames, prev_fg, depth_valid, sketch.T)
 
 
 def local(frames, prev_fg, depth_valid, sketch, tv_weight):
     count, chans, rows, cols = frames.shape
     strips = lax.axis_size("pix")
     nval = chans * rows * strips * cols
-    swapped, gram, frames, ok = gram_of(frames, prev_fg, depth_valid)
-    weights = mixing_of(gram, sketch, nval)
-    back, fore = finish_of(swapped, weights, frames, ok, tv_weight, cols)
-
-    def unflat(value):
-        return value.reshape(chans, count, rows, cols).transpose(1, 0, 2, 3)
-
-    return unflat(back), unflat(fore)
+    return low_rank_and_rest(frames, prev_fg, depth_valid, sketch, tv_weight, nval)
 
 
 def solution(mesh):

time: 104 us -> 102 us (0.981); the launches traced: 103 us -> 102 us
    transpose x1 -> x0, local copies, waits for them, and re-layouts: 2.65 us -> none  [unflat(): return value.reshape(chans, count, rows, cols).transpose(1, 0, 2, 3)]
    unnamed x8, local copies, waits for them, and re-layouts: 2.89 us -> 5.27 us
    pallas_call x3 -> x1, Pallas kernels: 96.8 us -> 96.3 us  [low_rank_and_rest(): pl.pallas_call(functools.partial(whole_kernel, nval), out_shape=(jax.Shap...]
where the time goes in v4:
time: 102 us
  Pallas kernels  96.3 us (94%)
  local copies, waits for them, and re-layouts  5.27 us (5%)
    pallas_call x1, Pallas kernels, low_rank_and_rest(): pl.pallas_call(functools.partial(whole_kernel, nval), out_shape=(jax.Shap...  96.3 us
    unnamed x8, local copies, waits for them, and re-layouts  5.27 us

profile of v4, /device:TPU:6, one launch (start us, length us, event | category | flops | bytes accessed | tf_op | source)
XLA Modules:
  0.0 102.2 jit_solution(10977559515105020762)
XLA Ops:
  0.6 0.0 copy-start
  0.6 1.2 %copy-done = s32[32,16,512]{2,1,0:T(8,128)S(1)} copy-done((s32[32,16,512]{2,1,0:T(8,128)S(1)}, s32[32,16,512]{2,1,0:T(8,128)}, u32[]{:S(2)}) %copy-start) | copy-done | bytes 1048600
  1.9 0.0 copy-start.1
  1.9 0.8 copy-done.1
  2.6 0.0 copy-start.2
  2.6 0.7 copy-done.2
  3.3 96.3 %godec.1 = (bf16[32,4,16,512]{3,2,1,0:T(8,128)(2,1)S(1)}, bf16[32,4,16,512]{3,2,1,0:T(8,128)(2,1)S(1)}) custom-call(f32[4]{0:T(128)S(1)} %copy-done.2, bf16[32,4,16,512]{3,2,1,0:T(8,128)(2,1)} %frames_hbm.1, bf16[32,4,16,512]{3,2,1,0:T(8,128)(2,1)} %prev_hbm.1, s32[32,16,512]{2,1,0:T(8,128)S(1)} %copy-done, f32[64,128]{1,0:T(8,128)S(1)} %bitcast.1), custom_call_target="tpu_custom_call" | custom-call | tf_op jit(solution)/shard_map/godec/pallas_call | solution.py:593
  99.5 1.3 %copy.9 = bf16[32,4,16,512]{3,2,1,0:T(8,128)(2,1)} copy(bf16[32,4,16,512]{3,2,1,0:T(8,128)(2,1)S(1)} %get-tuple-element.4) | data formatting | bytes 4194304
  100.9 1.3 %copy.10 = bf16[32,4,16,512]{3,2,1,0:T(8,128)(2,1)} copy(bf16[32,4,16,512]{3,2,1,0:T(8,128)(2,1)S(1)} %get-tuple-element.5) | data formatting | bytes 4194304
Async XLA Ops:
  0.6 1.2 %copy-start = (s32[32,16,512]{2,1,0:T(8,128)S(1)}, s32[32,16,512]{2,1,0:T(8,128)}, u32[]{:S(2)}) copy-start(s32[32,16,512]{2,1,0:T(8,128)} %depth_hbm.1) | copy-start | bytes 3145732
  1.9 0.8 copy-start.1
  2.6 0.7 copy-start.2

commit v5 on v4

--- a/solution.py
+++ b/solution.py
@@ -303,9 +303,8 @@
     return [jnp.concatenate(out, axis=0) for out in solved]
 
 
-def mixing_stage(gram, sketch, gram_sc, basis_sc):
+def mixing_stage(gram, gram_sc, basis_sc):
     gram_sc[...] = gram
-    basis_sc[...] = sketch
 
     def turn(step, carry):
         basis = basis_sc[...]
@@ -535,10 +534,22 @@
             halo(offset, way).wait_send()
 
 
-def whole_kernel(nval, lam_ref, frames_hbm, prev_hbm, depth_hbm, sketch, back, fore, *scratch):
+def whole_kernel(
+    nval, lam_hbm, frames_hbm, prev_hbm, depth_hbm, sketch_hbm, back, fore, lam_ref, small_sem,
+    *scratch
+):
     swapped, flat_frames, flat_valid = scratch[:3]
+    basis_sc = scratch[25]
+    small = [
+        pltpu.make_async_copy(lam_hbm, lam_ref, small_sem.at[0]),
+        pltpu.make_async_copy(sketch_hbm, basis_sc, small_sem.at[1]),
+    ]
+    for copy in small:
+        copy.start()
     gram = gram_stage(frames_hbm, prev_hbm, depth_hbm, *scratch[:24])
-    mix = mixing_stage(gram * (1.0 / nval), sketch[...], *scratch[24:26])
+    for copy in small:
+        copy.wait()
+    mix = mixing_stage(gram * (1.0 / nval), *scratch[24:26])
     finish_stage(
         lam_ref, swapped, mix, flat_frames, flat_valid, back, fore, scratch[7], *scratch[26:]
     )
@@ -593,16 +604,17 @@
     return pl.pallas_call(
         functools.partial(whole_kernel, nval),
         out_shape=(jax.ShapeDtypeStruct(frames.shape, BF16),) * 2,
-        in_specs=[pl.BlockSpec(memory_space=pltpu.SMEM)]
-        + [pl.BlockSpec(memory_space=pltpu.HBM)] * 3
-        + in_vmem(1),
+        in_specs=[pl.BlockSpec(memory_space=pltpu.HBM)] * 5,
         out_specs=tuple(in_vmem(2)),
-        scratch_shapes=gram_scratch + mixing_scratch + finish_scratch,
+        scratch_shapes=[pltpu.SMEM((chans,), F32), dma((2,))]
+        + gram_scratch
+        + mixing_scratch
+        + finish_scratch,
         compiler_params=pltpu.CompilerParams(
             collective_id=0, has_side_effects=True, vmem_limit_bytes=48 << 20
         ),
         name="godec",
-    )(lam, frames, prev_fg, depth_valid, sketch.T)
+    )(*[pltpu.with_memory_space_constraint(v, pltpu.HBM) for v in (lam, frames, prev_fg, depth_valid, sketch.T)])
 
 
 def local(frames, prev_fg, depth_valid, sketch, tv_weight):

time: 102 us -> 99.5 us (0.975)
  local copies, waits for them, and re-layouts: 5.27 us -> 2.64 us
    unnamed x8 -> x2, local copies, waits for them, and re-layouts: 5.27 us -> 2.64 us
where the time goes in v5:
time: 99.5 us; the launch traced here: 99.4 us
  Pallas kernels  96.1 us (97%)
  local copies, waits for them, and re-layouts  2.64 us (3%)
    pallas_call x1, Pallas kernels, low_rank_and_rest(): pl.pallas_call(functools.partial(whole_kernel, nval), out_shape=(jax.Shap...  96.1 us
    unnamed x2, local copies, waits for them, and re-layouts  2.64 us

profile of v5, /device:TPU:6, one launch (start us, length us, event | category | flops | bytes accessed | tf_op | source)
XLA Modules:
  0.0 99.4 jit_solution(7597361147420019386)
XLA Ops:
  0.6 96.1 %godec.1 = (bf16[32,4,16,512]{3,2,1,0:T(8,128)(2,1)S(1)}, bf16[32,4,16,512]{3,2,1,0:T(8,128)(2,1)S(1)}) custom-call(f32[4]{0:T(128)} %lam_hbm.1, bf16[32,4,16,512]{3,2,1,0:T(8,128)(2,1)} %frames_hbm.1, bf16[32,4,16,512]{3,2,1,0:T(8,128)(2,1)} %prev_hbm.1, s32[32,16,512]{2,1,0:T(8,128)} %depth_hbm.1, f32[64,128]{1,0:T(8,128)} %bitcast.1), custom_call_target="tpu_custom_call" | custom-call | tf_op jit(solution)/shard_map/godec/pallas_call | solution.py:604
  96.8 1.3 %copy.9 = bf16[32,4,16,512]{3,2,1,0:T(8,128)(2,1)} copy(bf16[32,4,16,512]{3,2,1,0:T(8,128)(2,1)S(1)} %get-tuple-element.4) | data formatting | bytes 4194304
  98.1 1.3 %copy.10 = bf16[32,4,16,512]{3,2,1,0:T(8,128)(2,1)} copy(bf16[32,4,16,512]{3,2,1,0:T(8,128)(2,1)S(1)} %get-tuple-element.5) | data formatting | bytes 4194304

commit v6 on v5

--- a/solution.py
+++ b/solution.py
@@ -75,8 +75,8 @@
 
 
 def gram_stage(
-    frames_hbm, prev_hbm, depth_hbm, swapped, flat_frames, flat_valid, frames, prev, depth, flat, lines, part, pieces, in_y, in_z, total,
-    load_sem, swap_send, swap_recv, first_send, first_recv, y_send, y_recv, z_send, z_recv,
+    frames_hbm, prev_hbm, depth_hbm, swapped, flat_frames, flat_valid, frames, prev, depth, flat, lines, part, pieces, in_plane, total,
+    load_sem, swap_send, swap_recv, first_send, first_recv, plane_send, plane_recv,
     last_send, last_recv,
 ):
     x, strip, y, z, core = place()
@@ -98,15 +98,13 @@
     def of_group(k):
         return (lax.div(k, 2), strip - core + lax.rem(k, 2))
 
-    def of_y(k):
-        return (x, (k * 4 + z) * 2 + core)
-
-    def of_z(k):
-        return (x, (y * 4 + k) * 2 + core)
+    plane = y * 4 + z
+
+    def of_plane(k):
+        return (x, k * 2 + core)
 
     partners = [of_group(wrap(group + k, 8)) for k in range(1, 8)]
-    partners += [of_y(wrap(y + k, 4)) for k in range(1, 4)]
-    partners += [of_z(wrap(z + k, 4)) for k in range(1, 4)]
+    partners += [of_plane(wrap(plane + k, 16)) for k in range(1, 16)]
     strips = lax.axis_size("pix")
     partners += [(x, wrap(strip + k, strips)) for k in (-1, 1)]
     barrier = pltpu.get_barrier_semaphore()
@@ -219,15 +217,11 @@
     copies = exchange(*args)
     pieces[group] = part[group]
     arrive(*args, copies)
-    in_y[y] = added(pieces, 8)
-
-    args = (y, 4, of_y, lambda k: in_y.at[y], in_y, y_send, y_recv)
+    in_plane[plane] = added(pieces, 8)
+
+    args = (plane, 16, of_plane, lambda k: in_plane.at[plane], in_plane, plane_send, plane_recv)
     arrive(*args, exchange(*args))
-    in_z[z] = added(in_y, 4)
-
-    args = (z, 4, of_z, lambda k: in_z.at[z], in_z, z_send, z_recv)
-    arrive(*args, exchange(*args))
-    total[group] = added(in_z, 4)
+    total[group] = added(in_plane, 16)
 
     args = (group, 8, of_group, lambda k: total.at[group], total, last_send, last_recv)
     arrive(*args, exchange(*args))
@@ -323,7 +317,7 @@
 
 def smooth_channel(
     strips, strip, chan, offset, lam_ref, frames, back, valid, above, below,
-    back_out, fore_out, lines_out, source, first, second, between,
+    back_out, fore_out, lines_out, source, first, second, edges_here, between,
 ):
     lam = lam_ref[chan]
     step = STEP_SIZE / lam
@@ -352,9 +346,6 @@
             value = lines_out[j].reshape(lines, rows, 128).astype(BF16)
             target[:, chan, :, 128 * j : 128 * j + 128] = value
 
-    for r in range(halo):
-        source[r] = above[offset, :, r * cols : (r + 1) * cols].astype(F32) * step
-        source[halo + rows + r] = below[offset, :, r * cols : (r + 1) * cols].astype(F32) * step
     for r in range(rows):
         where = slice(r * cols, (r + 1) * cols)
         ok = jnp.where(chan == last, valid[:, where].astype(F32), 1.0)
@@ -362,6 +353,10 @@
         unturn(r, [held[:, 128 * j : 128 * j + 128] for j in range(tiles)])
         source[halo + r] = (frames[chan, :, where].astype(F32) - held) * (ok * step)
     unlay(back_out)
+    edges_here()
+    for r in range(halo):
+        source[r] = above[offset, :, r * cols : (r + 1) * cols].astype(F32) * step
+        source[halo + rows + r] = below[offset, :, r * cols : (r + 1) * cols].astype(F32) * step
 
     def before(values):
         turned = [pltpu.roll(v, 1, 1) for v in values]
@@ -486,10 +481,10 @@
 
     multiply(0)
     multiply(1)
-    forward(0)
     for offset in (1, 3):
         for part in range(2):
             send(offset, part).start()
+    forward(0)
     multiply(2)
     for offset in (1, 3):
         send(offset, 2).start()
@@ -506,8 +501,9 @@
         def _():
             taken(offset, 2).wait_recv()
 
-        for way in range(2):
-            halo(offset, way).wait_recv()
+        def edges_here():
+            for way in range(2):
+                halo(offset, way).wait_recv()
 
         def between(sweep):
             for turn, at, offsets in ((0, 3, (1, 3)), (2, 1, (2,))):
@@ -521,7 +517,7 @@
         smooth_channel(
             strips, strip, wrap(x - offset, SIDE), offset, lam_ref,
             frames, back, valid, above, below, back_out, fore_out, lines_out,
-            source, first, second, between,
+            source, first, second, edges_here, between,
         )
         return carry
 
@@ -539,19 +535,19 @@
     *scratch
 ):
     swapped, flat_frames, flat_valid = scratch[:3]
-    basis_sc = scratch[25]
+    basis_sc = scratch[22]
     small = [
         pltpu.make_async_copy(lam_hbm, lam_ref, small_sem.at[0]),
         pltpu.make_async_copy(sketch_hbm, basis_sc, small_sem.at[1]),
     ]
     for copy in small:
         copy.start()
-    gram = gram_stage(frames_hbm, prev_hbm, depth_hbm, *scratch[:24])
+    gram = gram_stage(frames_hbm, prev_hbm, depth_hbm, *scratch[:21])
     for copy in small:
         copy.wait()
-    mix = mixing_stage(gram * (1.0 / nval), *scratch[24:26])
+    mix = mixing_stage(gram * (1.0 / nval), *scratch[21:23])
     finish_stage(
-        lam_ref, swapped, mix, flat_frames, flat_valid, back, fore, scratch[7], *scratch[26:]
+        lam_ref, swapped, mix, flat_frames, flat_valid, back, fore, scratch[7], *scratch[23:]
     )
 
 
@@ -576,14 +572,12 @@
         VMEM((cols // 128, count * rows, 128), F32),
         VMEM((8, piece, every), F32),
         VMEM((8, piece, every), F32),
-        VMEM((4, piece, every), F32),
-        VMEM((4, piece, every), F32),
+        VMEM((16, piece, every), F32),
         VMEM((8, piece, every), F32),
         dma((2 * chans + 1,)),
         dma((4, 2)), dma((4, 2)),
         dma((8,)), dma((8,)),
-        dma((4,)), dma((4,)),
-        dma((4,)), dma((4,)),
+        dma((16,)), dma((16,)),
         dma((8,)), dma((8,)),
     ]
     mixing_scratch = [VMEM((every, every), F32), VMEM((rank, every), F32)]

time: 99.5 us -> 98 us (0.985)
  Pallas kernels: 96.1 us -> 94.6 us
    pallas_call x1, Pallas kernels: 96.1 us -> 94.6 us  [low_rank_and_rest(): pl.pallas_call(functools.partial(whole_kernel, nval), out_shape=(jax.Shap...]
where the time goes in v6:
time: 98 us; the launch traced here: 97.9 us
  Pallas kernels  94.6 us (97%)
  local copies, waits for them, and re-layouts  2.64 us (3%)
    pallas_call x1, Pallas kernels, low_rank_and_rest(): pl.pallas_call(functools.partial(whole_kernel, nval), out_shape=(jax.Shap...  94.6 us
    unnamed x2, local copies, waits for them, and re-layouts  2.64 us

profile of v6, /device:TPU:6, one launch (start us, length us, event | category | flops | bytes accessed | tf_op | source)
XLA Modules:
  0.0 97.9 jit_solution(3640471008601384016)
XLA Ops:
  0.6 94.6 %godec.1 = (bf16[32,4,16,512]{3,2,1,0:T(8,128)(2,1)S(1)}, bf16[32,4,16,512]{3,2,1,0:T(8,128)(2,1)S(1)}) custom-call(f32[4]{0:T(128)} %lam_hbm.1, bf16[32,4,16,512]{3,2,1,0:T(8,128)(2,1)} %frames_hbm.1, bf16[32,4,16,512]{3,2,1,0:T(8,128)(2,1)} %prev_hbm.1, s32[32,16,512]{2,1,0:T(8,128)} %depth_hbm.1, f32[64,128]{1,0:T(8,128)} %bitcast.1), custom_call_target="tpu_custom_call" | custom-call | tf_op jit(solution)/shard_map/godec/pallas_call | solution.py:598
  95.3 1.3 %copy.9 = bf16[32,4,16,512]{3,2,1,0:T(8,128)(2,1)} copy(bf16[32,4,16,512]{3,2,1,0:T(8,128)(2,1)S(1)} %get-tuple-element.4) | data formatting | bytes 4194304
  96.6 1.3 %copy.10 = bf16[32,4,16,512]{3,2,1,0:T(8,128)(2,1)} copy(bf16[32,4,16,512]{3,2,1,0:T(8,128)(2,1)S(1)} %get-tuple-element.5) | data formatting | bytes 4194304

commit v7 on v6

--- a/solution.py
+++ b/solution.py
@@ -122,7 +122,9 @@
 
     args = (x, strip, flat, swapped, swap_send, swap_recv)
     pixels = rows * cols
-    halves = (pl.ds(0, pixels // 2), pl.ds(pixels // 2, pixels // 2))
+    count_parts = 4
+    span = pixels // count_parts
+    halves = [pl.ds(k * span, span) for k in range(count_parts)]
     sends = []
     first.wait()
     for k, offset in enumerate(ORDER):
@@ -137,9 +139,10 @@
             pl.semaphore_wait(barrier, len(partners))
         sends.append(send_along_x(*args, offset, 0, halves[0]))
         sends[-1].start()
-    for offset in ORDER:
-        sends.append(send_along_x(*args, offset, 1, halves[1]))
-        sends[-1].start()
+    for part_of in range(1, count_parts):
+        for offset in ORDER:
+            sends.append(send_along_x(*args, offset, part_of, halves[part_of]))
+            sends[-1].start()
     for copy in loads[-1]:
         copy.wait()
 
@@ -164,10 +167,10 @@
     every = count * SIDE
     chunk = 1024
     partial = jnp.zeros((every, every), F32)
-    for half in range(2):
+    for half in range(count_parts):
         for offset in ORDER:
             taken_along_x(*args, offset, half, halves[half]).wait_recv()
-        for start in range(half * pixels // 2, (half + 1) * pixels // 2, chunk):
+        for start in range(half * span, (half + 1) * span, chunk):
             block = swapped[:, :, start : start + chunk].reshape(every, chunk)
             partial = partial + lax.dot_general(
                 block, block, (((1,), (1,)), ((), ())), preferred_element_type=F32
@@ -575,7 +578,7 @@
         VMEM((16, piece, every), F32),
         VMEM((8, piece, every), F32),
         dma((2 * chans + 1,)),
-        dma((4, 2)), dma((4, 2)),
+        dma((4, 4)), dma((4, 4)),
         dma((8,)), dma((8,)),
         dma((16,)), dma((16,)),
         dma((8,)), dma((8,)),

time: 98 us -> 97.9 us (level)
  no operation moved by 1% of the time
where the time goes in v7:
time: 97.9 us; the launch traced here: 97.8 us
  Pallas kernels  94.5 us (97%)
  local copies, waits for them, and re-layouts  2.64 us (3%)
    pallas_call x1, Pallas kernels, low_rank_and_rest(): pl.pallas_call(functools.partial(whole_kernel, nval), out_shape=(jax.Shap...  94.5 us
    unnamed x2, local copies, waits for them, and re-layouts  2.64 us

profile of v7, /device:TPU:6, one launch (start us, length us, event | category | flops | bytes accessed | tf_op | source)
XLA Modules:
  0.0 97.8 jit_solution(10933314395826339048)
XLA Ops:
  0.6 94.5 %godec.1 = (bf16[32,4,16,512]{3,2,1,0:T(8,128)(2,1)S(1)}, bf16[32,4,16,512]{3,2,1,0:T(8,128)(2,1)S(1)}) custom-call(f32[4]{0:T(128)} %lam_hbm.1, bf16[32,4,16,512]{3,2,1,0:T(8,128)(2,1)} %frames_hbm.1, bf16[32,4,16,512]{3,2,1,0:T(8,128)(2,1)} %prev_hbm.1, s32[32,16,512]{2,1,0:T(8,128)} %depth_hbm.1, f32[64,128]{1,0:T(8,128)} %bitcast.1), custom_call_target="tpu_custom_call" | custom-call | tf_op jit(solution)/shard_map/godec/pallas_call | solution.py:601
  95.2 1.3 %copy.9 = bf16[32,4,16,512]{3,2,1,0:T(8,128)(2,1)} copy(bf16[32,4,16,512]{3,2,1,0:T(8,128)(2,1)S(1)} %get-tuple-element.4) | data formatting | bytes 4194304
  96.5 1.3 %copy.10 = bf16[32,4,16,512]{3,2,1,0:T(8,128)(2,1)} copy(bf16[32,4,16,512]{3,2,1,0:T(8,128)(2,1)S(1)} %get-tuple-element.5) | data formatting | bytes 4194304
